TPU v7x, 32 devices: a whole 2x2x4 slice. The times are simulated.
32 devices in a mesh: ctx: 16 (over z, y, x), wt: 2 (over core).
Axes of the slice: x: 2, y: 2, z: 4, core: 2. Of those that a mesh axis runs over, the one named last changes fastest.
Arguments:
- block_input: bfloat16 [4, 2304, 768], P('wt', 'ctx'), may hold values from -6 to 6
- span_order: int32 [16, 2], replicated, may hold values from 0 to 31, as said below
- doc_lengths: int32 [4, 4], P('wt'), may hold values from 1 to 1152, 2304 in all within a row
- ln1_gain: bfloat16 [768], P('wt'), may hold values from 0.5 to 1.5
- ln1_bias: bfloat16 [768], P('wt'), may hold values from -1.796875 to 1.796875
- w_qkv: bfloat16 [768, 2304], P('wt'), may hold values from -0.21875 to 0.21875
- qv_bias: bfloat16 [2, 768], P(None, 'wt'), may hold values from -0.59765625 to 0.59765625
- w_out: bfloat16 [768, 768], P('wt'), may hold values from -12 to 12
- out_bias: bfloat16 [768], P('wt'), may hold values from -6 to 6
- ln2_gain: bfloat16 [768], P('wt'), may hold values from 0.5 to 1.5
- ln2_bias: bfloat16 [768], P('wt'), may hold values from -1.796875 to 1.796875
- w_fc: bfloat16 [768, 3072], P('wt'), may hold values from -0.21875 to 0.21875
- fc_bias: bfloat16 [3072], P('wt'), may hold values from -3 to 3
- w_proj: bfloat16 [3072, 768], P('wt'), may hold values from -0.75 to 0.75
- proj_bias: bfloat16 [768], P('wt'), may hold values from -6 to 6
- d_out: bfloat16 [4, 2304, 768], P('wt', 'ctx'), may hold values from -6 to 6
Outputs:
- block_out: bfloat16 [4, 2304, 768], P('wt', 'ctx')
- d_input: float32 [4, 2304, 768], P('wt', 'ctx')
- grad_ln1_gain: float32 [768], P('wt')
- grad_ln1_bias: float32 [768], P('wt')
- grad_w_qkv: float32 [768, 2304], P('wt')
- grad_qv_bias: float32 [2, 768], P(None, 'wt')
- grad_w_out: float32 [768, 768], P('wt')
- grad_out_bias: float32 [768], P('wt')
- grad_ln2_gain: float32 [768], P('wt')
- grad_ln2_bias: float32 [768], P('wt')
- grad_w_fc: float32 [768, 3072], P('wt')
- grad_fc_bias: float32 [3072], P('wt')
- grad_w_proj: float32 [3072, 768], P('wt')
- grad_proj_bias: float32 [768], P('wt')
Inputs may be any that keep to these rules, and one draw needn't show every extreme that they name: `span_order`: row i names two spans j and 31 - j, in either order; every span of 0 to 31 is named exactly once. `doc_lengths`: each row sums to 2304, and its largest entry is 1152.
All inputs are finite; a program needn't handle non-finite values.
Results may differ from a plain program's by a relative error of at most 0.015.
Values may be sent and summed in bfloat16 or wider, within the bound.
No kernel may reach another device: no remote copies, remote signals or barrier semaphores. Data moves between devices by JAX's collectives and lax.ppermute only.
A program may use at most 320 MiB of HBM per device.

v0:
```python
import jax
import jax.numpy as jnp
from jax import lax
from jax.sharding import PartitionSpec as P

HEADS = 12


branch_scale = 0.14433756729740643
neg_large = -1e30


def layer_norm(values, gain, shift):
    center = jnp.mean(values, axis=-1, keepdims=True)
    moved = values - center
    spread = jnp.mean(moved * moved, axis=-1, keepdims=True)
    return moved * lax.rsqrt(spread + 1e-05) * gain + shift


def gelu_tanh(values):
    return (
        0.5
        * values
        * (1.0 + jnp.tanh(0.7978845608028654 * (values + 0.044715 * values * values * values)))
    )


def split_count(row_total, limit):
    pieces = 1
    while row_total % pieces != 0 or row_total // pieces > limit:
        pieces += 1
    return pieces


def row_positions(order_table, first_index, row_total, seq_dev, span_rows):
    rows_here = first_index + jnp.arange(row_total, dtype=jnp.int32)
    device_of = rows_here // seq_dev
    half_of = rows_here % seq_dev // span_rows
    slot_index = device_of * 2 + half_of
    flat_order = order_table.reshape(-1)
    table_slots = jnp.arange(flat_order.shape[0], dtype=jnp.int32)
    picked = jnp.sum(
        jnp.where(slot_index[:, None] == table_slots[None, :], flat_order[None, :], 0), axis=1
    )
    return picked * span_rows + rows_here % span_rows


def doc_of(positions, lengths_row):
    ends_at = jnp.cumsum(lengths_row)
    inner_ends = ends_at[:-1]
    return jnp.sum((positions[:, None] >= inner_ends[None, :]).astype(jnp.int32), axis=1)


def visible(query_pos, query_doc, key_pos, key_doc):
    causal = key_pos[None, None, :] <= query_pos[None, :, None]
    same_doc = key_doc[:, None, :] == query_doc[:, :, None]
    return (causal & same_doc)[:, :, None, :]


def per_device(
    block_input,
    span_order,
    doc_lengths,
    ln1_gain,
    ln1_bias,
    w_qkv,
    qv_bias,
    w_out,
    out_bias,
    ln2_gain,
    ln2_bias,
    w_fc,
    fc_bias,
    w_proj,
    proj_bias,
    d_out,
):
    seq_group, seq_dev, width = block_input.shape
    heads = HEADS
    head_dim = width // heads
    span_rows = seq_dev // 2
    score_scale = head_dim ** (-0.5)

    def docs_for(positions):
        return jax.vmap(doc_of, in_axes=(None, 0))(positions, doc_lengths)

    weights_all = (
        lax.all_gather(ln1_gain, "wt", axis=0, tiled=True),
        lax.all_gather(ln1_bias, "wt", axis=0, tiled=True),
        lax.all_gather(w_qkv, "wt", axis=0, tiled=True),
        lax.all_gather(qv_bias, "wt", axis=1, tiled=True),
        lax.all_gather(w_out, "wt", axis=0, tiled=True),
        lax.all_gather(out_bias, "wt", axis=0, tiled=True),
        lax.all_gather(ln2_gain, "wt", axis=0, tiled=True),
        lax.all_gather(ln2_bias, "wt", axis=0, tiled=True),
        lax.all_gather(w_fc, "wt", axis=0, tiled=True),
        lax.all_gather(fc_bias, "wt", axis=0, tiled=True),
        lax.all_gather(w_proj, "wt", axis=0, tiled=True),
        lax.all_gather(proj_bias, "wt", axis=0, tiled=True),
    )
    gain_one = weights_all[0].astype(jnp.float32)
    shift_one = weights_all[1].astype(jnp.float32)
    bias_pair = weights_all[3].astype(jnp.float32)
    bias_out = weights_all[5].astype(jnp.float32)
    gain_two = weights_all[6].astype(jnp.float32)
    shift_two = weights_all[7].astype(jnp.float32)
    bias_fc = weights_all[9].astype(jnp.float32)
    bias_proj = weights_all[11].astype(jnp.float32)
    me_ctx = lax.axis_index("ctx")
    local_pos = row_positions(span_order, me_ctx * seq_dev, seq_dev, seq_dev, span_rows)
    local_doc = docs_for(local_pos)
    tokens_in = block_input.astype(jnp.float32)
    normed_one = layer_norm(tokens_in, gain_one, shift_one).astype(jnp.bfloat16)
    qkv_bias = jnp.concatenate([bias_pair[0], jnp.zeros((width,), jnp.float32), bias_pair[1]])
    projected = (
        jnp.einsum("btd,de->bte", normed_one, weights_all[2], preferred_element_type=jnp.float32)
        + qkv_bias
    )
    projected_low = projected.astype(jnp.bfloat16)
    query_low = projected_low[..., :width]
    key_low = projected_low[..., width : 2 * width]
    value_low = projected_low[..., 2 * width :]
    query_heads = query_low.reshape(seq_group, seq_dev, heads, head_dim)
    key_heads = key_low.reshape(seq_group, seq_dev, heads, head_dim)
    value_heads = value_low.reshape(seq_group, seq_dev, heads, head_dim)
    start_state = (
        jnp.zeros((seq_group, seq_dev, heads, head_dim), jnp.float32),
        jnp.full((seq_group, seq_dev, heads), neg_large, jnp.float32),
        jnp.zeros((seq_group, seq_dev, heads), jnp.float32),
    )
    key_piece = lax.all_gather(key_low, "ctx", axis=1, tiled=True)
    value_piece = lax.all_gather(value_low, "ctx", axis=1, tiled=True)
    piece_rows = key_piece.shape[1]
    key_pos = row_positions(span_order, jnp.int32(0), piece_rows, seq_dev, span_rows)
    key_doc = docs_for(key_pos)
    block_rows = piece_rows // split_count(piece_rows, 1024)

    def one_block(block_index, running):
        acc_sum, run_max, run_total = running
        first_row = block_index * block_rows
        key_block = lax.dynamic_slice_in_dim(key_piece, first_row, block_rows, 1).reshape(
            seq_group, block_rows, heads, head_dim
        )
        value_block = lax.dynamic_slice_in_dim(value_piece, first_row, block_rows, 1).reshape(
            seq_group, block_rows, heads, head_dim
        )
        allowed = visible(
            local_pos,
            local_doc,
            lax.dynamic_slice_in_dim(key_pos, first_row, block_rows, 0),
            lax.dynamic_slice_in_dim(key_doc, first_row, block_rows, 1),
        )
        scores = (
            jnp.einsum(
                "bqhd,bkhd->bqhk", query_heads, key_block, preferred_element_type=jnp.float32
            )
            * score_scale
        )
        scores = jnp.where(allowed, scores, neg_large)
        new_max = jnp.maximum(run_max, jnp.max(scores, axis=-1))
        weights = jnp.where(allowed, jnp.exp(scores - new_max[..., None]), 0.0)
        rescale = jnp.exp(run_max - new_max)
        run_total = run_total * rescale + jnp.sum(weights, axis=-1)
        acc_sum = acc_sum * rescale[..., None] + jnp.einsum(
            "bqhk,bkhd->bqhd",
            weights.astype(jnp.bfloat16),
            value_block,
            preferred_element_type=jnp.float32,
        )
        return (acc_sum, new_max, run_total)

    acc_sum, run_max, run_total = lax.fori_loop(0, piece_rows // block_rows, one_block, start_state)
    attn_heads = acc_sum / run_total[..., None]
    log_total = run_max + jnp.log(run_total)
    attn_out = attn_heads.reshape(seq_group, seq_dev, width)
    attn_low = attn_out.astype(jnp.bfloat16)
    branch_pre = (
        jnp.einsum("btd,de->bte", attn_low, weights_all[4], preferred_element_type=jnp.float32)
        + bias_out
    )
    resid_one = tokens_in + branch_scale * branch_pre
    normed_two = layer_norm(resid_one, gain_two, shift_two).astype(jnp.bfloat16)
    hidden_pre = (
        jnp.einsum("btd,df->btf", normed_two, weights_all[8], preferred_element_type=jnp.float32)
        + bias_fc
    )
    hidden_low = gelu_tanh(hidden_pre).astype(jnp.bfloat16)
    mlp_pre = (
        jnp.einsum("btf,fd->btd", hidden_low, weights_all[10], preferred_element_type=jnp.float32)
        + bias_proj
    )
    block_out = (resid_one + branch_scale * mlp_pre).astype(jnp.bfloat16)
    weights_back = (
        lax.all_gather(ln1_gain, "wt", axis=0, tiled=True),
        lax.all_gather(ln1_bias, "wt", axis=0, tiled=True),
        lax.all_gather(w_qkv, "wt", axis=0, tiled=True),
        lax.all_gather(qv_bias, "wt", axis=1, tiled=True),
        lax.all_gather(w_out, "wt", axis=0, tiled=True),
        lax.all_gather(out_bias, "wt", axis=0, tiled=True),
        lax.all_gather(ln2_gain, "wt", axis=0, tiled=True),
        lax.all_gather(ln2_bias, "wt", axis=0, tiled=True),
        lax.all_gather(w_fc, "wt", axis=0, tiled=True),
        lax.all_gather(fc_bias, "wt", axis=0, tiled=True),
        lax.all_gather(w_proj, "wt", axis=0, tiled=True),
        lax.all_gather(proj_bias, "wt", axis=0, tiled=True),
    )
    back_gain_one = weights_back[0].astype(jnp.float32)
    back_shift_one = weights_back[1].astype(jnp.float32)
    back_gain_two = weights_back[6].astype(jnp.float32)
    back_shift_two = weights_back[7].astype(jnp.float32)
    cotangent = d_out.astype(jnp.float32)
    d_mlp = (branch_scale * cotangent).astype(jnp.bfloat16)
    grad_w_proj = jnp.einsum("btf,btd->fd", hidden_low, d_mlp, preferred_element_type=jnp.float32)
    grad_proj_bias = jnp.sum(d_mlp.astype(jnp.float32), axis=(0, 1))
    d_hidden = jnp.einsum(
        "btd,fd->btf", d_mlp, weights_back[10], preferred_element_type=jnp.float32
    )
    gelu_unused, gelu_pull = jax.vjp(gelu_tanh, hidden_pre)
    d_pre = gelu_pull(d_hidden)[0].astype(jnp.bfloat16)
    grad_w_fc = jnp.einsum("btd,btf->df", normed_two, d_pre, preferred_element_type=jnp.float32)
    grad_fc_bias = jnp.sum(d_pre.astype(jnp.float32), axis=(0, 1))
    d_normed_two = jnp.einsum(
        "btf,df->btd", d_pre, weights_back[8], preferred_element_type=jnp.float32
    )
    norm_unused, norm_pull = jax.vjp(layer_norm, resid_one, back_gain_two, back_shift_two)
    d_resid_part, grad_ln2_gain, grad_ln2_bias = norm_pull(d_normed_two)
    d_resid = cotangent + d_resid_part
    d_branch = (branch_scale * d_resid).astype(jnp.bfloat16)
    grad_w_out = jnp.einsum("btd,bte->de", attn_low, d_branch, preferred_element_type=jnp.float32)
    grad_out_bias = jnp.sum(d_branch.astype(jnp.float32), axis=(0, 1))
    d_attn_low = jnp.einsum(
        "bte,de->btd", d_branch, weights_back[4], preferred_element_type=jnp.float32
    ).astype(jnp.bfloat16)
    d_attn_heads = d_attn_low.reshape(seq_group, seq_dev, heads, head_dim)
    delta = jnp.sum(d_attn_heads.astype(jnp.float32) * attn_heads, axis=-1)
    fold_key_piece = lax.all_gather(key_low, "ctx", axis=1, tiled=True)
    fold_value_piece = lax.all_gather(value_low, "ctx", axis=1, tiled=True)
    piece_rows = fold_key_piece.shape[1]
    fold_key_pos = row_positions(span_order, jnp.int32(0), piece_rows, seq_dev, span_rows)
    fold_key_doc = docs_for(fold_key_pos)
    fold_block_rows = piece_rows // split_count(piece_rows, 1024)

    def one_block(block_index, grad_query):
        first_row = block_index * fold_block_rows
        key_block = lax.dynamic_slice_in_dim(fold_key_piece, first_row, fold_block_rows, 1).reshape(
            seq_group, fold_block_rows, heads, head_dim
        )
        value_block = lax.dynamic_slice_in_dim(
            fold_value_piece, first_row, fold_block_rows, 1
        ).reshape(seq_group, fold_block_rows, heads, head_dim)
        allowed = visible(
            local_pos,
            local_doc,
            lax.dynamic_slice_in_dim(fold_key_pos, first_row, fold_block_rows, 0),
            lax.dynamic_slice_in_dim(fold_key_doc, first_row, fold_block_rows, 1),
        )
        scores = (
            jnp.einsum(
                "bqhd,bkhd->bqhk", query_heads, key_block, preferred_element_type=jnp.float32
            )
            * score_scale
        )
        probs = jnp.where(allowed, jnp.exp(scores - log_total[..., None]), 0.0)
        d_probs = jnp.einsum(
            "bqhd,bkhd->bqhk", d_attn_heads, value_block, preferred_element_type=jnp.float32
        )
        d_scores = (probs * (d_probs - delta[..., None])).astype(jnp.bfloat16)
        return (
            grad_query
            + jnp.einsum("bqhk,bkhd->bqhd", d_scores, key_block, preferred_element_type=jnp.float32)
            * score_scale
        )

    grad_query = lax.fori_loop(
        0,
        piece_rows // fold_block_rows,
        one_block,
        jnp.zeros((seq_group, seq_dev, heads, head_dim), jnp.float32),
    )
    stats_all = (
        lax.all_gather(log_total, "ctx", axis=1, tiled=True),
        lax.all_gather(delta, "ctx", axis=1, tiled=True),
    )
    totals_every = stats_all[0]
    deltas_every = stats_all[1]

    def fold_keys(carried, received, first_index):
        query_piece, grad_piece = received
        piece_rows = query_piece.shape[1]
        query_pos = row_positions(span_order, first_index, piece_rows, seq_dev, span_rows)
        query_doc = docs_for(query_pos)
        block_rows = piece_rows // split_count(piece_rows, 1024)

        def one_block(block_index, running):
            grad_key, grad_value = running
            first_row = block_index * block_rows
            query_block = lax.dynamic_slice_in_dim(query_piece, first_row, block_rows, 1).reshape(
                seq_group, block_rows, heads, head_dim
            )
            grad_block = lax.dynamic_slice_in_dim(grad_piece, first_row, block_rows, 1).reshape(
                seq_group, block_rows, heads, head_dim
            )
            total_block = lax.dynamic_slice_in_dim(totals_every, first_row, block_rows, 1)
            delta_block = lax.dynamic_slice_in_dim(deltas_every, first_row, block_rows, 1)
            allowed = visible(
                lax.dynamic_slice_in_dim(query_pos, first_row, block_rows, 0),
                lax.dynamic_slice_in_dim(query_doc, first_row, block_rows, 1),
                local_pos,
                local_doc,
            )
            scores = (
                jnp.einsum(
                    "bqhd,bkhd->bqhk", query_block, key_heads, preferred_element_type=jnp.float32
                )
                * score_scale
            )
            probs = jnp.where(allowed, jnp.exp(scores - total_block[..., None]), 0.0)
            grad_value = grad_value + jnp.einsum(
                "bqhk,bqhd->bkhd",
                probs.astype(jnp.bfloat16),
                grad_block,
                preferred_element_type=jnp.float32,
            )
            d_probs = jnp.einsum(
                "bqhd,bkhd->bqhk", grad_block, value_heads, preferred_element_type=jnp.float32
            )
            d_scores = (probs * (d_probs - delta_block[..., None])).astype(jnp.bfloat16)
            grad_key = (
                grad_key
                + jnp.einsum(
                    "bqhk,bqhd->bkhd", d_scores, query_block, preferred_element_type=jnp.float32
                )
                * score_scale
            )
            return (grad_key, grad_value)

        return lax.fori_loop(0, piece_rows // block_rows, one_block, carried)

    zero_heads = jnp.zeros((seq_group, seq_dev, heads, head_dim), jnp.float32)
    grad_key, grad_value = fold_keys(
        (zero_heads, zero_heads),
        (
            lax.all_gather(query_low, "ctx", axis=1, tiled=True),
            lax.all_gather(d_attn_low, "ctx", axis=1, tiled=True),
        ),
        jnp.int32(0),
    )
    d_projected = jnp.concatenate(
        [
            grad_query.reshape(seq_group, seq_dev, width),
            grad_key.reshape(seq_group, seq_dev, width),
            grad_value.reshape(seq_group, seq_dev, width),
        ],
        axis=-1,
    ).astype(jnp.bfloat16)
    grad_w_qkv = jnp.einsum(
        "btd,bte->de", normed_one, d_projected, preferred_element_type=jnp.float32
    )
    column_sums = jnp.sum(d_projected.astype(jnp.float32), axis=(0, 1))
    grad_qv_bias = jnp.stack([column_sums[:width], column_sums[2 * width :]])
    d_normed_one = jnp.einsum(
        "bte,de->btd", d_projected, weights_back[2], preferred_element_type=jnp.float32
    )
    first_unused, first_pull = jax.vjp(layer_norm, tokens_in, back_gain_one, back_shift_one)
    d_input_part, grad_ln1_gain, grad_ln1_bias = first_pull(d_normed_one)
    d_input = d_resid + d_input_part
    shares = (
        lax.psum_scatter(
            grad_ln1_gain.astype(jnp.bfloat16), "wt", scatter_dimension=0, tiled=True
        ).astype(jnp.float32),
        lax.psum_scatter(
            grad_ln1_bias.astype(jnp.bfloat16), "wt", scatter_dimension=0, tiled=True
        ).astype(jnp.float32),
        lax.psum_scatter(
            grad_w_qkv.astype(jnp.bfloat16), "wt", scatter_dimension=0, tiled=True
        ).astype(jnp.float32),
        lax.psum_scatter(
            grad_qv_bias.astype(jnp.bfloat16), "wt", scatter_dimension=1, tiled=True
        ).astype(jnp.float32),
        lax.psum_scatter(
            grad_w_out.astype(jnp.bfloat16), "wt", scatter_dimension=0, tiled=True
        ).astype(jnp.float32),
        lax.psum_scatter(
            grad_out_bias.astype(jnp.bfloat16), "wt", scatter_dimension=0, tiled=True
        ).astype(jnp.float32),
        lax.psum_scatter(
            grad_ln2_gain.astype(jnp.bfloat16), "wt", scatter_dimension=0, tiled=True
        ).astype(jnp.float32),
        lax.psum_scatter(
            grad_ln2_bias.astype(jnp.bfloat16), "wt", scatter_dimension=0, tiled=True
        ).astype(jnp.float32),
        lax.psum_scatter(
            grad_w_fc.astype(jnp.bfloat16), "wt", scatter_dimension=0, tiled=True
        ).astype(jnp.float32),
        lax.psum_scatter(
            grad_fc_bias.astype(jnp.bfloat16), "wt", scatter_dimension=0, tiled=True
        ).astype(jnp.float32),
        lax.psum_scatter(
            grad_w_proj.astype(jnp.bfloat16), "wt", scatter_dimension=0, tiled=True
        ).astype(jnp.float32),
        lax.psum_scatter(
            grad_proj_bias.astype(jnp.bfloat16), "wt", scatter_dimension=0, tiled=True
        ).astype(jnp.float32),
    )
    totals = lax.psum(
        (
            shares[0],
            shares[1],
            shares[2],
            shares[3],
            shares[4],
            shares[5],
            shares[6],
            shares[7],
            shares[8],
            shares[9],
            shares[10],
            shares[11],
        ),
        "ctx",
    )
    return (
        block_out,
        d_input,
        totals[0],
        totals[1],
        totals[2],
        totals[3],
        totals[4],
        totals[5],
        totals[6],
        totals[7],
        totals[8],
        totals[9],
        totals[10],
        totals[11],
    )


def solution(mesh):
    placed = (
        P("wt", "ctx", None),
        P(),
        P("wt", None),
        P("wt"),
        P("wt"),
        P("wt", None),
        P(None, "wt"),
        P("wt", None),
        P("wt"),
        P("wt"),
        P("wt"),
        P("wt", None),
        P("wt"),
        P("wt", None),
        P("wt"),
        P("wt", "ctx", None),
    )
    return jax.shard_map(
        per_device,
        mesh=mesh,
        in_specs=placed,
        out_specs=(
            P("wt", "ctx", None),
            P("wt", "ctx", None),
            P("wt"),
            P("wt"),
            P("wt", None),
            P(None, "wt"),
            P("wt", None),
            P("wt"),
            P("wt"),
            P("wt"),
            P("wt", None),
            P("wt"),
            P("wt", None),
            P("wt"),
        ),
        check_vma=False,
    )
```

profile of v0, /device:TPU:0, one launch (start us, length us, event | category | flops | bytes accessed | tf_op | source)
XLA Modules:
  0.0 1320.7 jit_solution(14129734389578113325)
XLA Ops:
  18.1 6.9 all-gather.16.cloned.1.call-done
  40.9 91.3 %all-gather.18.cloned.1.call-done = bf16[2,2304,768]{2,1,0:T(8,128)(2,1)} async-done(((bf16[2,144,768]{2,1,0:T(8,128)(2,1)}), bf16[2,2304,768]{2,1,0:T(8,128)(2,1)}) %all-gather.18.cloned.1.call-update) | async-done | bytes 7077904 | tf_op jit(solution)/shard_map/all_gather | solution.py:131
  132.2 10.4 copy.110
  142.6 92.3 %all-gather.20.cloned.1.call-done = bf16[2,2304,768]{2,1,0:T(8,128)(2,1)} async-done(((bf16[2,144,768]{2,1,0:T(8,128)(2,1)}), bf16[2,2304,768]{2,1,0:T(8,128)(2,1)}) %all-gather.20.cloned.1.call-update) | async-done | bytes 7077904 | tf_op jit(solution)/shard_map/all_gather | solution.py:132
  235.0 10.1 copy.111
  245.1 67.5 %while.48 = (s32[]{:T(128)}, f32[2,144,12,64]{1,3,2,0:T(8,128)}, f32[2,144,12]{1,2,0:T(8,128)S(1)}, f32[2,144,12]{1,2,0:T(8,128)S(1)}, s32[2304]{0:T(1024)S(1)},...) while((s32[]{:T(128)}, f32[2,144,12,64]{1,3,2,0:T(8,128)}, ...), condition=%wide.region_10.11_spmd.clone, body=%wide.region_7.10_spmd.clone.sunk | while | flops 715215744 | bytes 92042152 | solution.py:172
  248.3 7.1 fusion.190
  255.4 7.3 fusion.191
  271.7 6.3 fusion.190
  278.1 6.9 fusion.191
  293.9 6.1 fusion.190
  300.0 6.9 fusion.191
  317.0 5.8 fusion.57
  322.9 8.8 fusion.140
  340.6 6.0 bitcast_convert_fusion.1
  355.2 58.2 %while.49 = (s32[]{:T(128)}, f32[2,144,12,64]{1,3,2,0:T(8,128)}, bf16[2,2304,768]{1,2,0:T(8,128)(2,1)}, s32[2304]{0:T(1024)S(1)}, s32[144]{0:T(256)S(1)}, /*inde...) while((s32[]{:T(128)}, f32[2,144,12,64]{1,3,2,0:T(8,128)}, ...), condition=%wide.region_17.18_spmd.clone, body=%wide.region_16.17_spmd.clone.sunk | while | flops 1036357632 | bytes 41123736 | solution.py:274
  365.4 9.2 bitcast_add_fusion.9
  384.8 9.2 bitcast_add_fusion.9
  404.2 9.3 bitcast_add_fusion.9
  416.0 88.6 %all_gather.79 = f32[2,2304,12]{2,0,1:T(2,128)S(1)} all-gather(f32[2,144,12]{2,0,1:T(2,128)S(1)} %copy-done.17), channel_id=1, replica_groups=mesh['ctx'=16,'wt'=2] {'ctx'}, dimensions={1}, use_global_device_ids=true | all-gather | bytes 235008 | tf_op jit(solution)/shard_map/all_gather | solution.py:282
  507.4 66.6 %all_gather.77 = f32[2,2304,12]{2,0,1:T(2,128)S(1)} all-gather(f32[2,144,12]{2,0,1:T(2,128)S(1)} %copy-done.14), channel_id=1, replica_groups=mesh['ctx'=16,'wt'=2] {'ctx'}, dimensions={1}, use_global_device_ids=true | all-gather | bytes 235008 | tf_op jit(solution)/shard_map/all_gather | solution.py:281
  577.2 7.3 bitcast_convert_fusion
  585.6 111.8 %while.50 = (s32[]{:T(128)}, f32[2,144,12,64]{1,3,2,0:T(8,128)}, f32[2,144,12,64]{1,3,2,0:T(8,128)}, bf16[2,2304,768]{2,1,0:T(8,128)(2,1)}, s32[144]{0:T(256)S(1...) while((s32[]{:T(128)}, f32[2,144,12,64]{1,3,2,0:T(8,128)}, ...), condition=%wide.region_19.20_spmd.clone, body=%wide.region_18.19_spmd.clone.sunk | while | flops 1387155456 | bytes 66016164 | solution.py:337
  605.8 8.2 bitcast_add_fusion.11
  613.9 8.8 bitcast_add_fusion.10
  631.0 5.6 fusion.208
  642.5 8.6 bitcast_add_fusion.11
  651.1 9.0 bitcast_add_fusion.10
  679.8 8.6 bitcast_add_fusion.11
  688.4 9.0 bitcast_add_fusion.10
  710.8 6.4 fusion.86
  730.6 583.4 %all-reduce.10 = (f32[384]{0:T(512)}, f32[384]{0:T(512)}, f32[384,2304]{1,0:T(8,128)}, f32[2,384]{1,0:T(2,128)}, f32[384,768]{1,0:T(8,128)}, /*index=5*/f32[384]...) all-reduce(f32[384]{0:T(512)S(1)} %get-tuple-element.1050, ...), channel_id=1, replica_groups=mesh['ctx'=16,'wt'=2] {'ctx'}, use_global_device_ids=true, to_apply=%region_24.25 | all-reduce | flops 3543552 | bytes 21268992 | tf_op jit(solution)/shard_map/psum | solution.py:405
  (297 shorter events, 194.2 us)
Async XLA Ops:
  7.2 17.8 %all-gather.16.cloned.1.call-start = ((), (), s32[]{:S(2)}) async-start(), calls=%async_computation.5 | async-start | bytes 5308416 | tf_op jit(solution)/shard_map/all_gather | solution.py:90
  7.9 124.3 %all-gather.18.cloned.1.call-start = ((), (), s32[]{:S(2)}) async-start(), calls=%async_computation.6 | async-start | bytes 7520256 | tf_op jit(solution)/shard_map/all_gather | solution.py:131
  10.6 14.4 %copy-start.18 = (f32[768]{0:T(1024)}, f32[768]{0:T(1024)S(1)}, u32[]{:S(2)}) copy-start(f32[768]{0:T(1024)S(1)} %reshape.382) | copy-start | bytes 9220
  15.0 10.0 copy-start.27
  16.3 8.8 copy-start.20
  18.1 6.9 copy-start.22
  29.5 11.2 copy-start.6
  29.5 6.7 copy-start.34
  29.5 8.5 copy-start.29
  29.5 205.4 %all-gather.20.cloned.1.call-start = ((), (), s32[]{:S(2)}) async-start(), calls=%async_computation.7 | async-start | bytes 7520256 | tf_op jit(solution)/shard_map/all_gather | solution.py:132
  30.3 284.0 %all-gather.22.cloned.1.call-start = ((), (), s32[]{:S(2)}) async-start(), calls=%async_computation.8 | async-start | bytes 1769472 | tf_op jit(solution)/shard_map/all_gather | solution.py:92
  30.9 286.1 %all-gather.24.cloned.1.call-start = ((), (), s32[]{:S(2)}) async-start(), calls=%async_computation.9 | async-start | bytes 7077888 | tf_op jit(solution)/shard_map/all_gather | solution.py:96
  31.4 291.4 %all-gather.26.cloned.1.call-start = ((), (), s32[]{:S(2)}) async-start(), calls=%async_computation.10 | async-start | bytes 7077888 | tf_op jit(solution)/shard_map/all_gather | solution.py:98
  32.0 552.6 %all-gather.28.cloned.1.call-start = ((), (), s32[]{:S(2)}) async-start(), calls=%async_computation.11 | async-start | bytes 7520256 | tf_op jit(solution)/shard_map/all_gather | solution.py:343
  40.7 543.9 %all-gather.30.cloned.1.call-start = ((), (), s32[]{:S(2)}) async-start(), calls=%async_computation.12 | async-start | bytes 7520256 | tf_op jit(solution)/shard_map/all_gather | solution.py:344
  255.4 8.1 copy-start
  278.1 7.2 copy-start
  300.0 7.2 copy-start
  316.7 23.9 %copy-start.8 = (f32[2,144,768]{2,1,0:T(8,128)}, f32[2,144,768]{2,1,0:T(8,128)S(1)}, u32[]{:S(2)}) copy-start(f32[2,144,768]{2,1,0:T(8,128)S(1)} %get-tuple-element.1040) | copy-start | bytes 2654212
  317.0 5.8 copy-start.11
  322.9 8.8 copy-start.36
  334.4 6.1 copy-start.26
  337.5 379.6 %reduce-scatter.10.cloned.1.call-start = ((), (), s32[]{:S(2)}) async-start(), calls=%async_computation.14 | async-start | bytes 1769472 | tf_op jit(solution)/shard_map/reduce_scatter | solution.py:380
  340.5 376.6 %reduce-scatter.12.cloned.1.call-start = ((), (), s32[]{:S(2)}) async-start(), calls=%async_computation.15 | async-start | bytes 7077888 | tf_op jit(solution)/shard_map/reduce_scatter | solution.py:392
  346.6 6.3 copy-start.5
  346.7 370.5 %reduce-scatter.14.cloned.1.call-start = ((), (), s32[]{:S(2)}) async-start(), calls=%async_computation.16 | async-start | bytes 7077888 | tf_op jit(solution)/shard_map/reduce_scatter | solution.py:398
  415.0 92.4 %copy-start.14 = (f32[2,144,12]{2,0,1:T(2,128)S(1)}, f32[2,144,12]{2,0,1:T(2,128)}, u32[]{:S(2)}) copy-start(f32[2,144,12]{2,0,1:T(2,128)} %copy-done.13) | copy-start | bytes 41476
  504.6 72.6 %copy-start.12 = (bf16[2,144,768]{2,1,0:T(8,128)(2,1)S(1)}, bf16[2,144,768]{2,1,0:T(8,128)(2,1)}, u32[]{:S(2)}) copy-start(bf16[2,144,768]{2,1,0:T(8,128)(2,1)} %param.37) | copy-start | bytes 1327108
  584.5 145.0 %reduce-scatter.16.cloned.1.call-start = ((), (), s32[]{:S(2)}) async-start(), calls=%async_computation.17 | async-start | bytes 294912
  702.2 28.3 %reduce-scatter.8.cloned.1.call-start = ((), (), s32[]{:S(2)}) async-start(), calls=%async_computation.13 | async-start | bytes 5308416 | tf_op jit(solution)/shard_map/reduce_scatter | solution.py:374
  717.1 10.1 copy-start.3
  722.3 8.2 copy-start.16
  (23 other events, 64.3 us)
Sparse Core Ops, SparseCore 0:
  9.6 15.3 all-gather.15
  29.7 102.4 all-gather.17
  135.5 99.4 all-gather.19
  236.4 7.3 all-gather.21
  245.2 15.6 all-gather.23
  262.3 15.6 all-gather.25
  280.6 102.5 all-gather.27
  385.9 134.4 all-gather.29
  523.3 10.5 reduce-scatter.9
  536.7 13.7 reduce-scatter.11
  584.7 11.4 reduce-scatter.13
  702.3 6.3 reduce-scatter.15
  711.1 12.4 reduce-scatter.7
where the time goes:
time: 1340 us; the launch traced here: 1320 us
  blocking collectives  757 us (56%)
  matrix products  204 us (15%)
  waiting for transfers between devices  194 us (14%)
  local copies, waits for them, and re-layouts  108 us (8%)
  other arithmetic  40.3 us (3%)
  between operations  16.1 us (1%)
    psum x1, blocking collectives, per_device(): lax.psum((shares[0], shares[1], shares[2], shares[3], shares[4], shares[5...  583 us
    all_gather x1, waiting for transfers between devices, per_device(): value_piece = lax.all_gather(value_low, 'ctx', axis=1, tiled=True)  92.3 us
    all_gather x1, waiting for transfers between devices, per_device(): key_piece = lax.all_gather(key_low, 'ctx', axis=1, tiled=True)  91.3 us
    all_gather x1, blocking collectives, per_device(): lax.all_gather(delta, 'ctx', axis=1, tiled=True)  88.6 us
    all_gather x1, blocking collectives, per_device(): lax.all_gather(log_total, 'ctx', axis=1, tiled=True)  66.6 us
    dot_general x6, matrix products, one_block(): jnp.einsum('bqhd,bkhd->bqhk', query_heads, key_block, preferred_element_t...  36.3 us
    unnamed x94, local copies, waits for them, and re-layouts  33.8 us
    dot_general x3, matrix products, one_block(): jnp.einsum('bqhk,bkhd->bqhd', d_scores, key_block, preferred_element_type...  27.7 us
  transfers between devices with their start and end apart: 13, of which 3 were waited for; matrix products, arithmetic and copies ran while one was open for 26% of the time, Pallas kernels for 0%

commit v1 on v0

--- a/solution.py
+++ b/solution.py
@@ -1,13 +1,514 @@
+import functools
+
 import jax
 import jax.numpy as jnp
 from jax import lax
+from jax.experimental import pallas as pl
+from jax.experimental.pallas import tpu as pltpu
 from jax.sharding import PartitionSpec as P
 
 HEADS = 12
-
 
 branch_scale = 0.14433756729740643
 neg_large = -1e30
+f32 = jnp.float32
+bf16 = jnp.bfloat16
+VMEM = pltpu.VMEM
+vmem_cap = 56 << 20
+
+GROUPS = 4
+TILE = 128
+PAD = 256
+
+pair = [(0, 1), (1, 0)]
+x_pairs = [(i, i ^ 1) for i in range(16)]
+y_pairs = [(i, i ^ 2) for i in range(16)]
+
+
+def z_shift(step):
+    return [(i, (i // 4 + step) % 4 * 4 + i % 4) for i in range(16)]
+
+
+def other_core(value):
+    return lax.ppermute(value, "wt", pair)
+
+
+def send_x(value):
+    return lax.ppermute(value, "ctx", x_pairs)
+
+
+def send_y(value):
+    return lax.ppermute(value, "ctx", y_pairs)
+
+
+def send_z(value, step):
+    return lax.ppermute(value, "ctx", z_shift(step))
+
+
+def row(value, index):
+    return lax.dynamic_index_in_dim(value, index, 0, keepdims=False)
+
+
+def sum_low(*terms):
+    total = terms[0].astype(f32)
+    for term in terms[1:]:
+        total = total + term.astype(f32)
+    return total.astype(bf16)
+
+
+def full_spec(shape):
+    zeros = (0,) * len(shape)
+    return pl.BlockSpec(shape, lambda *unused: zeros)
+
+
+def dot(left, right, dims):
+    return lax.dot_general(left, right, (dims, ((), ())), preferred_element_type=f32)
+
+
+def norm_parts(rows):
+    center = jnp.mean(rows, axis=-1, keepdims=True)
+    moved = rows - center
+    spread = jnp.mean(moved * moved, axis=-1, keepdims=True)
+    inverse = lax.rsqrt(spread + 1e-05)
+    return moved * inverse, inverse
+
+
+def project_kernel(
+    order_ref, a_ref, b_ref, c_ref, d_ref, gain_ref, shift_ref, weight_ref, bias_ref,
+    h_ref, q_ref, kv_ref,
+):
+    rows = jnp.concatenate([r[0].astype(f32) for r in (a_ref, b_ref, c_ref, d_ref)], axis=0)
+    normed, unused = norm_parts(rows)
+    low = (normed * gain_ref[...] + shift_ref[...]).astype(bf16)
+    h_ref[...] = low
+    out = dot(low, weight_ref[...], ((1,), (0,))) + bias_ref[...]
+    q_ref[...] = (out[:, :PAD].astype(bf16) * 0.125).astype(bf16)
+    kv_ref[...] = out[:, PAD:].astype(bf16)
+
+
+def span_specs(span_rows, width):
+    return [
+        pl.BlockSpec((1, span_rows, width), lambda i, order, t=t: (order[4 * i + t], 0, 0))
+        for t in range(4)
+    ]
+
+
+def project(order, pieces, gain, shift, weight, bias):
+    spans, span_rows, width = pieces.shape
+    rows = spans * span_rows
+    step = 4 * span_rows
+    grid_spec = pltpu.PrefetchScalarGridSpec(
+        num_scalar_prefetch=1,
+        grid=(spans // 4,),
+        in_specs=span_specs(span_rows, width)
+        + [
+            full_spec((1, width)),
+            full_spec((1, width)),
+            full_spec((width, 3 * PAD)),
+            full_spec((1, 3 * PAD)),
+        ],
+        out_specs=[
+            pl.BlockSpec((step, width), lambda i, order: (i, 0)),
+            pl.BlockSpec((step, PAD), lambda i, order: (i, 0)),
+            pl.BlockSpec((step, 2 * PAD), lambda i, order: (i, 0)),
+        ],
+    )
+    return pl.pallas_call(
+        project_kernel,
+        grid_spec=grid_spec,
+        out_shape=[
+            jax.ShapeDtypeStruct((rows, width), bf16),
+            jax.ShapeDtypeStruct((rows, PAD), bf16),
+            jax.ShapeDtypeStruct((rows, 2 * PAD), bf16),
+        ],
+        compiler_params=pltpu.CompilerParams(vmem_limit_bytes=vmem_cap),
+        cost_estimate=pl.CostEstimate(
+            flops=2 * rows * width * 3 * PAD, bytes_accessed=6 << 20, transcendentals=0
+        ),
+        name="project",
+    )(order, pieces, pieces, pieces, pieces, gain, shift, weight, bias)
+
+
+def by_head(tile):
+    lane = lax.broadcasted_iota(jnp.int32, tile.shape, 1)
+    zero = jnp.zeros_like(tile)
+    return jnp.concatenate(
+        [jnp.where((lane >= 64 * h) & (lane < 64 * h + 64), tile, zero) for h in range(3)], axis=0
+    )
+
+
+def visible_tile(kpos_ref, tile_row, meta_ref):
+    rows = pl.ds(tile_row, TILE)
+    keys = jnp.concatenate([kpos_ref[0, rows, :], kpos_ref[1, rows, :]], axis=0)
+    return (keys <= meta_ref[0, 0:1, :]) & (keys >= meta_ref[0, 1:2, :])
+
+
+def attend_kernel(
+    low_ref, high_ref, slot_ref, q_ref, own_ref, oth_ref, kpos_ref, meta_ref,
+    o_ref, lse_ref, out_ref,
+    vown, voth, stack, acc, top,
+):
+    i = pl.program_id(0)
+    spans, span_rows, feats = out_ref.shape
+
+    @pl.when(i == 0)
+    def _():
+        vown[...] = own_ref[:, PAD:].T
+        voth[...] = oth_ref[:, PAD:].T
+
+    stack[...] = by_head(q_ref[...])
+    acc[...] = jnp.zeros_like(acc)
+    top[...] = jnp.full_like(top, neg_large)
+
+    def one(j, carry):
+        first = pl.multiple_of(j * TILE, TILE)
+        rows = pl.ds(first, TILE)
+        keys = jnp.concatenate([own_ref[rows, :PAD], oth_ref[rows, :PAD]], axis=0)
+        scores = dot(keys, stack[...], ((1,), (1,)))
+        allowed = visible_tile(kpos_ref, first, meta_ref)
+        allowed = jnp.concatenate([allowed, allowed, allowed], axis=1)
+        scores = jnp.where(allowed, scores, neg_large)
+        old = top[...]
+        new = jnp.maximum(old, jnp.max(scores, axis=0, keepdims=True))
+        probs = jnp.exp(scores - new).astype(bf16)
+        vals = jnp.concatenate([vown[:, rows], voth[:, rows]], axis=1)
+        acc[...] = acc[...] * jnp.exp(old - new) + dot(vals, probs, ((1,), (0,)))
+        top[...] = new
+        return carry
+
+    lax.fori_loop(low_ref[i], high_ref[i], one, 0)
+    total = acc[192:193, :]
+    lse_ref[0] = top[...] + jnp.log(total)
+    parts = [
+        acc[64 * h : 64 * h + 64, TILE * h : TILE * h + TILE] / total[:, TILE * h : TILE * h + TILE]
+        for h in range(3)
+    ]
+    heads_t = jnp.concatenate(parts + [jnp.zeros((64, TILE), f32)], axis=0)
+    o_ref[pl.ds(pl.multiple_of(i * TILE, TILE), TILE), :] = heads_t.T
+
+    @pl.when(i == pl.num_programs(0) - 1)
+    def _():
+        for a in range(spans):
+            out_ref[slot_ref[a]] = o_ref[span_rows * a : span_rows * (a + 1), :feats].astype(bf16)
+
+
+def attend(low, high, slot, q, own, oth, kpos, meta, spans):
+    rows = q.shape[0]
+    tiles = rows // TILE
+    wide = 3 * TILE
+    grid_spec = pltpu.PrefetchScalarGridSpec(
+        num_scalar_prefetch=3,
+        grid=(tiles,),
+        in_specs=[
+            pl.BlockSpec((TILE, PAD), lambda i, *unused: (i, 0)),
+            full_spec((rows, 2 * PAD)),
+            full_spec((rows, 2 * PAD)),
+            full_spec((2, rows, TILE)),
+            pl.BlockSpec((1, 2, TILE), lambda i, *unused: (i, 0, 0)),
+        ],
+        out_specs=[
+            full_spec((rows, PAD)),
+            pl.BlockSpec((1, 1, wide), lambda i, *unused: (i, 0, 0)),
+            full_spec((spans, rows // spans, 192)),
+        ],
+        scratch_shapes=[
+            VMEM((PAD, rows), bf16),
+            VMEM((PAD, rows), bf16),
+            VMEM((wide, PAD), bf16),
+            VMEM((PAD, wide), f32),
+            VMEM((1, wide), f32),
+        ],
+    )
+    return pl.pallas_call(
+        attend_kernel,
+        grid_spec=grid_spec,
+        out_shape=[
+            jax.ShapeDtypeStruct((rows, PAD), f32),
+            jax.ShapeDtypeStruct((tiles, 1, wide), f32),
+            jax.ShapeDtypeStruct((spans, rows // spans, 192), bf16),
+        ],
+        compiler_params=pltpu.CompilerParams(vmem_limit_bytes=vmem_cap),
+        cost_estimate=pl.CostEstimate(
+            flops=2 * wide * rows * PAD * tiles, bytes_accessed=8 << 20, transcendentals=rows * rows
+        ),
+        name="attend",
+    )(low, high, slot, q, own, oth, kpos, meta)
+
+
+def attend_back_kernel(
+    low_ref, high_ref, slot_ref, q_ref, own_ref, oth_ref, kpos_ref, meta_ref, grad_ref, o_ref, lse_ref,
+    dq_ref, down_ref, doth_ref,
+    grads, kown, koth, acc_own, acc_oth, stack, gstack, dq_t,
+):
+    i = pl.program_id(0)
+    spans, span_rows, feats = grad_ref.shape
+
+    @pl.when(i == 0)
+    def _():
+        kown[...] = own_ref[:, :PAD].T
+        koth[...] = oth_ref[:, :PAD].T
+        acc_own[...] = jnp.zeros_like(acc_own)
+        acc_oth[...] = jnp.zeros_like(acc_oth)
+        grads[...] = jnp.zeros_like(grads)
+        for a in range(spans):
+            grads[span_rows * a : span_rows * (a + 1), :feats] = grad_ref[slot_ref[a]].astype(f32)
+
+    here = pl.ds(pl.multiple_of(i * TILE, TILE), TILE)
+    grad = grads[here, :]
+    stack[...] = by_head(q_ref[...])
+    gstack[...] = by_head(grad.astype(bf16))
+    product = (grad * o_ref[...]).T
+    delta = jnp.concatenate(
+        [jnp.sum(product[64 * h : 64 * h + 64], axis=0, keepdims=True) for h in range(3)], axis=1
+    )
+    lse = lse_ref[0]
+    dq_t[...] = jnp.zeros_like(dq_t)
+
+    def one(j, carry):
+        first = pl.multiple_of(j * TILE, TILE)
+        rows = pl.ds(first, TILE)
+        keys = jnp.concatenate([own_ref[rows, :PAD], oth_ref[rows, :PAD]], axis=0)
+        vals = jnp.concatenate([own_ref[rows, PAD:], oth_ref[rows, PAD:]], axis=0)
+        scores = dot(keys, stack[...], ((1,), (1,)))
+        allowed = visible_tile(kpos_ref, first, meta_ref)
+        allowed = jnp.concatenate([allowed, allowed, allowed], axis=1)
+        probs = jnp.where(allowed, jnp.exp(scores - lse), 0.0)
+        d_probs = dot(vals, gstack[...], ((1,), (1,)))
+        d_scores = (probs * (d_probs - delta)).astype(bf16)
+        d_vals = dot(probs.astype(bf16), gstack[...], ((1,), (0,)))
+        d_keys = dot(d_scores, stack[...], ((1,), (0,)))
+        acc_own[rows, :PAD] += d_keys[:TILE]
+        acc_own[rows, PAD:] += d_vals[:TILE]
+        acc_oth[rows, :PAD] += d_keys[TILE:]
+        acc_oth[rows, PAD:] += d_vals[TILE:]
+        keys_t = jnp.concatenate([kown[:, rows], koth[:, rows]], axis=1)
+        dq_t[...] += dot(keys_t, d_scores, ((1,), (0,)))
+        return carry
+
+    lax.fori_loop(low_ref[i], high_ref[i], one, 0)
+    parts = [dq_t[64 * h : 64 * h + 64, TILE * h : TILE * h + TILE] for h in range(3)]
+    heads_t = jnp.concatenate(parts + [jnp.zeros((64, TILE), f32)], axis=0) * 0.125
+    dq_ref[...] = heads_t.T.astype(bf16)
+
+    @pl.when(i == pl.num_programs(0) - 1)
+    def _():
+        down_ref[...] = acc_own[...]
+        doth_ref[...] = acc_oth[...].astype(bf16)
+
+
+def attend_back(low, high, slot, q, own, oth, kpos, meta, grad, o, lse):
+    rows = q.shape[0]
+    tiles = rows // TILE
+    wide = 3 * TILE
+    grid_spec = pltpu.PrefetchScalarGridSpec(
+        num_scalar_prefetch=3,
+        grid=(tiles,),
+        in_specs=[
+            pl.BlockSpec((TILE, PAD), lambda i, *unused: (i, 0)),
+            full_spec((rows, 2 * PAD)),
+            full_spec((rows, 2 * PAD)),
+            full_spec((2, rows, TILE)),
+            pl.BlockSpec((1, 2, TILE), lambda i, *unused: (i, 0, 0)),
+            full_spec(grad.shape),
+            pl.BlockSpec((TILE, PAD), lambda i, *unused: (i, 0)),
+            pl.BlockSpec((1, 1, wide), lambda i, *unused: (i, 0, 0)),
+        ],
+        out_specs=[
+            pl.BlockSpec((TILE, PAD), lambda i, *unused: (i, 0)),
+            full_spec((rows, 2 * PAD)),
+            full_spec((rows, 2 * PAD)),
+        ],
+        scratch_shapes=[
+            VMEM((rows, PAD), f32),
+            VMEM((PAD, rows), bf16),
+            VMEM((PAD, rows), bf16),
+            VMEM((rows, 2 * PAD), f32),
+            VMEM((rows, 2 * PAD), f32),
+            VMEM((wide, PAD), bf16),
+            VMEM((wide, PAD), bf16),
+            VMEM((PAD, wide), f32),
+        ],
+    )
+    return pl.pallas_call(
+        attend_back_kernel,
+        grid_spec=grid_spec,
+        out_shape=[
+            jax.ShapeDtypeStruct((rows, PAD), bf16),
+            jax.ShapeDtypeStruct((rows, 2 * PAD), f32),
+            jax.ShapeDtypeStruct((rows, 2 * PAD), bf16),
+        ],
+        compiler_params=pltpu.CompilerParams(vmem_limit_bytes=vmem_cap),
+        cost_estimate=pl.CostEstimate(
+            flops=5 * wide * rows * PAD * tiles, bytes_accessed=12 << 20, transcendentals=rows * rows
+        ),
+        name="attend_back",
+    )(low, high, slot, q, own, oth, kpos, meta, grad, o, lse)
+
+
+def unproject_kernel(
+    order_ref, a_ref, b_ref, c_ref, d_ref, dq_ref, down_ref, doth_ref, weight_ref,
+    pieces_ref, grad_ref, gain_ref, shift_ref, bias_ref,
+):
+    i = pl.program_id(0)
+    span_rows = a_ref.shape[1]
+
+    @pl.when(i == 0)
+    def _():
+        gain_ref[...] = jnp.zeros_like(gain_ref)
+        shift_ref[...] = jnp.zeros_like(shift_ref)
+        bias_ref[...] = jnp.zeros_like(bias_ref)
+
+    rows = jnp.concatenate([r[0].astype(f32) for r in (a_ref, b_ref, c_ref, d_ref)], axis=0)
+    normed, unused = norm_parts(rows)
+    dkv = (down_ref[...] + doth_ref[...].astype(f32)).astype(bf16)
+    grad = jnp.concatenate([dq_ref[...], dkv], axis=1)
+    grad_ref[...] = grad
+    bias_ref[...] += jnp.sum(grad.astype(f32), axis=0, keepdims=True)
+    back = dot(grad, weight_ref[...], ((1,), (1,)))
+    gain_ref[...] += jnp.sum(back * normed, axis=0, keepdims=True)
+    shift_ref[...] += jnp.sum(back, axis=0, keepdims=True)
+    for t in range(4):
+        pieces_ref[order_ref[4 * i + t]] = back[span_rows * t : span_rows * (t + 1)].astype(bf16)
+
+
+def unproject(order, pieces, dq, down, doth, weight):
+    spans, span_rows, width = pieces.shape
+    rows = spans * span_rows
+    step = 4 * span_rows
+    grid_spec = pltpu.PrefetchScalarGridSpec(
+        num_scalar_prefetch=1,
+        grid=(spans // 4,),
+        in_specs=span_specs(span_rows, width)
+        + [
+            pl.BlockSpec((step, PAD), lambda i, order: (i, 0)),
+            pl.BlockSpec((step, 2 * PAD), lambda i, order: (i, 0)),
+            pl.BlockSpec((step, 2 * PAD), lambda i, order: (i, 0)),
+            full_spec((width, 3 * PAD)),
+        ],
+        out_specs=[
+            full_spec(pieces.shape),
+            pl.BlockSpec((step, 3 * PAD), lambda i, order: (i, 0)),
+            full_spec((1, width)),
+            full_spec((1, width)),
+            full_spec((1, 3 * PAD)),
+        ],
+    )
+    return pl.pallas_call(
+        unproject_kernel,
+        grid_spec=grid_spec,
+        out_shape=[
+            jax.ShapeDtypeStruct(pieces.shape, bf16),
+            jax.ShapeDtypeStruct((rows, 3 * PAD), bf16),
+            jax.ShapeDtypeStruct((1, width), f32),
+            jax.ShapeDtypeStruct((1, width), f32),
+            jax.ShapeDtypeStruct((1, 3 * PAD), f32),
+        ],
+        compiler_params=pltpu.CompilerParams(vmem_limit_bytes=vmem_cap),
+        cost_estimate=pl.CostEstimate(
+            flops=2 * rows * width * 3 * PAD, bytes_accessed=9 << 20, transcendentals=0
+        ),
+        name="unproject",
+    )(order, pieces, pieces, pieces, pieces, dq, down, doth, weight)
+
+
+def reduce_plane(value, bits, sends):
+    for bit, send in zip(bits, sends):
+        value = value.reshape(2, value.shape[0] // 2, value.shape[1])
+        value = sum_low(row(value, bit), send(row(value, 1 - bit)))
+    return value
+
+
+def reduce_z(value, z):
+    value = value.reshape(4, value.shape[0] // 4, value.shape[1])
+    got = [send_z(row(value, (z + k) % 4), k) for k in (1, 2, 3)]
+    return sum_low(row(value, z), *got)
+
+
+def reduce_pair(left, right, where):
+    z, y, x = where
+    left = reduce_plane(left, (x, y), (send_x, send_y))
+    right = reduce_plane(right, (y, x), (send_y, send_x))
+    both = reduce_z(jnp.concatenate([left, right], axis=1), z)
+    return both
+
+
+def gather_pair(both, where):
+    half = both.shape[1] // 2
+    stack = jnp.stack([both] + [send_z(both, k) for k in (1, 2, 3)])
+    left, right = stack[:, :, :half], stack[:, :, half:]
+    left_y, left_x = send_y(left), send_x(left)
+    right_x, right_y = send_x(right), send_y(right)
+    return place_pair(
+        (left, left_x, left_y, send_x(left_y)), (right, right_x, right_y, send_y(right_x)), where
+    )
+
+
+def place_kernel(where_ref, *refs):
+    lefts, rights, out_ref = refs[:4], refs[4:8], refs[8]
+    z, y, x = where_ref[0], where_ref[1], where_ref[2]
+    rows, half = lefts[0].shape[1:]
+    for index in range(4):
+        part_x = x ^ (index & 1)
+        part_y = y ^ (index >> 1)
+        for k in range(4):
+            block_z = (z - k) & 3
+            at = pl.multiple_of(((part_x * 2 + part_y) * 4 + block_z) * rows, 8)
+            out_ref[pl.ds(at, rows), :half] = lefts[index][k].astype(f32)
+            at = pl.multiple_of(((part_y * 2 + part_x) * 4 + block_z) * rows, 8)
+            out_ref[pl.ds(at, rows), half:] = rights[index][k].astype(f32)
+
+
+def place_pair(lefts, rights, where):
+    blocks, rows, half = lefts[0].shape
+    shape = (16 * rows, 2 * half)
+    return pl.pallas_call(
+        place_kernel,
+        grid_spec=pltpu.PrefetchScalarGridSpec(
+            num_scalar_prefetch=1,
+            grid=(1,),
+            in_specs=[full_spec((blocks, rows, half))] * 8,
+            out_specs=full_spec(shape),
+        ),
+        out_shape=jax.ShapeDtypeStruct(shape, f32),
+        compiler_params=pltpu.CompilerParams(vmem_limit_bytes=vmem_cap),
+        cost_estimate=pl.CostEstimate(
+            flops=shape[0] * shape[1], bytes_accessed=6 * shape[0] * shape[1], transcendentals=0
+        ),
+        name="place",
+    )(jnp.stack(where).astype(jnp.int32), *lefts, *rights)
+
+
+def sum_everywhere(value):
+    value = value + other_core(value)
+    for send in (send_x, send_y):
+        value = value + send(value)
+    return value + send_z(value, 1) + send_z(value, 2) + send_z(value, 3)
+
+
+def split_halves(value, w, axis):
+    half = value.shape[axis] // 2
+    own = lax.dynamic_slice_in_dim(value, w * half, half, axis)
+    oth = lax.dynamic_slice_in_dim(value, (1 - w) * half, half, axis)
+    return own, oth
+
+
+def own_rows_sum(left, right, w):
+    own, oth = split_halves(left, w, 1)
+    got = other_core(dot(oth, right, ((0,), (0,))).astype(bf16))
+    return (dot(own, right, ((0,), (0,))) + got.astype(f32)).astype(bf16)
+
+
+def column_halves(value):
+    half = value.shape[1] // 2
+    return value[:, :half], value[:, half:]
+
+
+def gelu_tanh(values):
+    return (
+        0.5
+        * values
+        * (1.0 + jnp.tanh(0.7978845608028654 * (values + 0.044715 * values * values * values)))
+    )
 
 
 def layer_norm(values, gain, shift):
@@ -17,11 +518,260 @@
     return moved * lax.rsqrt(spread + 1e-05) * gain + shift
 
 
-def gelu_tanh(values):
+def norm_back(grad, rows, gain):
+    normed, inverse = norm_parts(rows)
+    scaled = grad * gain
+    part = scaled - jnp.mean(scaled, axis=-1, keepdims=True)
+    part = part - normed * jnp.mean(scaled * normed, axis=-1, keepdims=True)
+    return inverse * part, normed
+
+
+def by_owner(
+    block_input, span_order, doc_lengths, ln1_gain, ln1_bias, w_qkv, qv_bias, w_out, out_bias,
+    ln2_gain, ln2_bias, w_fc, fc_bias, w_proj, proj_bias, d_out,
+):
+    seq_group, seq_dev, width = block_input.shape
+    seqs = 2 * seq_group
+    span_rows = seq_dev // 2
+    chips = span_order.shape[0]
+    rows = chips * span_rows
+    me = lax.axis_index("ctx")
+    w = lax.axis_index("wt")
+    z, y, x = me // 4, me // 2 % 2, me % 2
+    where = (z, y, x)
+    group = me % 4
+
+    second = (row(span_order, me)[0] % 2) != w
+
+    def take_spans(value):
+        value = value.reshape(seq_group, 2, span_rows, width)
+        keep = jnp.where(second, value[:, 1], value[:, 0])
+        give = jnp.where(second, value[:, 0], value[:, 1])
+        got = other_core(give)
+        return jnp.where(
+            w == 0, jnp.concatenate([keep, got], axis=0), jnp.concatenate([got, keep], axis=0)
+        )
+
+    def give_spans(value):
+        low, high = value[:seq_group], value[seq_group:]
+        keep = jnp.where(w == 0, low, high)
+        got = other_core(jnp.where(w == 0, high, low))
+        first = jnp.where(second, got, keep)
+        last = jnp.where(second, keep, got)
+        return jnp.concatenate([first, last], axis=1)
+
+    tokens_low = take_spans(block_input)
+    kept = [row(tokens_low, z)] + [send_z(row(tokens_low, (z + k) % 4), k) for k in (1, 2, 3)]
+    left, right = jnp.stack(kept[:2]), jnp.stack(kept[2:])
+    left = jnp.concatenate([left, send_x(left)], axis=0)
+    right = jnp.concatenate([right, send_y(right)], axis=0)
+    pieces = jnp.concatenate([left, send_y(left), right, send_x(right)], axis=0)
+    cot_low = take_spans(d_out)
+
+    chip_ids = jnp.arange(chips, dtype=jnp.int32)
+    span_here = jnp.where(span_order[:, 0] % 2 == w, span_order[:, 0], span_order[:, 1]) // 2
+    span_ids = jnp.arange(chips, dtype=jnp.int32)
+    holder = jnp.sum(
+        jnp.where(span_here[None, :] == span_ids[:, None], chip_ids[None, :], 0), axis=1
+    ).astype(jnp.int32)
+    back_z = (z - holder // 4) % 4
+    flip_y = (y ^ (holder // 2 % 2)).astype(jnp.int32)
+    flip_x = (x ^ (holder % 2)).astype(jnp.int32)
+    order = jnp.where(
+        back_z < 2, flip_y * 4 + flip_x * 2 + back_z, 8 + flip_x * 4 + flip_y * 2 + back_z - 2
+    ).astype(jnp.int32)
+
+    lengths_oth = other_core(doc_lengths)
+    lengths = jnp.where(
+        w == 0,
+        jnp.concatenate([doc_lengths, lengths_oth], axis=0),
+        jnp.concatenate([lengths_oth, doc_lengths], axis=0),
+    )
+    lengths = row(lengths, z)
+    ends = jnp.cumsum(lengths)[:-1]
+    ranks = jnp.arange(rows, dtype=jnp.int32)
+    even_pos = 2 * span_rows * (ranks // span_rows) + ranks % span_rows
+    own_pos = even_pos + span_rows * w
+    oth_pos = even_pos + span_rows * (1 - w)
+    starts = jnp.sum(
+        jnp.where(own_pos[:, None] >= ends[None, :], lengths[None, :-1], 0), axis=1
+    ).astype(jnp.int32)
+    tiles = rows // TILE
+    own_tiles = own_pos.reshape(tiles, TILE)
+    start_tiles = starts.reshape(tiles, TILE)
+    meta = jnp.stack([own_tiles, start_tiles], axis=1).astype(jnp.int32)
+    kpos = jnp.broadcast_to(jnp.stack([own_pos, oth_pos])[:, :, None], (2, rows, TILE)).astype(jnp.int32)
+    even_tiles = even_pos.reshape(tiles, TILE)
+    low = jnp.sum(
+        (even_tiles[None, :, -1] + span_rows < start_tiles[:, 0:1]).astype(jnp.int32), axis=1
+    ).astype(jnp.int32)
+    high = jnp.sum(
+        (even_tiles[None, :, 0] <= own_tiles[:, -1:]).astype(jnp.int32), axis=1
+    ).astype(jnp.int32)
+
+    def join(own, axis=0):
+        got = other_core(own)
+        return jnp.where(
+            w == 0,
+            jnp.concatenate([own, got], axis=axis),
+            jnp.concatenate([got, own], axis=axis),
+        )
+
+    feats = width // GROUPS
+
+    def pad_cols(value, fill=0.0):
+        return jnp.pad(value, [(0, 0)] * (value.ndim - 1) + [(0, PAD - feats)], constant_values=fill)
+
+    columns = w_qkv.reshape(w_qkv.shape[0], 3, GROUPS, feats)
+    columns = lax.dynamic_index_in_dim(columns, group, 2, keepdims=False)
+    weight_in = join(pad_cols(columns).reshape(w_qkv.shape[0], 3 * PAD))
+    small = jnp.concatenate(
+        [ln1_gain, ln1_bias, qv_bias[0], qv_bias[1], out_bias, ln2_gain, ln2_bias, proj_bias, fc_bias]
+    )
+    small_oth = other_core(small)
+    small_pair = jnp.where(w == 0, jnp.stack([small, small_oth]), jnp.stack([small_oth, small])).astype(f32)
+    half = width // 2
+
+    def vector(index, size=half):
+        return small_pair[:, index * half : index * half + size].reshape(1, 2 * size)
+
+    gain_one, shift_one, bias_q, bias_v, bias_out, gain_two, shift_two, bias_proj = (
+        vector(i) for i in range(8)
+    )
+    bias_fc = vector(8, fc_bias.shape[0])
+    bias_q = lax.dynamic_slice_in_dim(bias_q, group * feats, feats, 1)
+    bias_v = lax.dynamic_slice_in_dim(bias_v, group * feats, feats, 1)
+    ones_tail = (jnp.arange(PAD) == feats).astype(f32)[None, :]
+    bias_in = jnp.concatenate(
+        [pad_cols(bias_q), jnp.zeros((1, PAD), f32), pad_cols(bias_v) + ones_tail], axis=1
+    )
+    weight_out = lax.all_gather(w_out, "wt", axis=0, tiled=True)
+    weight_fc = lax.all_gather(w_fc, "wt", axis=0, tiled=True)
+    weight_proj = lax.all_gather(w_proj, "wt", axis=0, tiled=True)
+
+    normed_one, query, kv_own = project(order, pieces, gain_one, shift_one, weight_in, bias_in)
+    kv_oth = other_core(kv_own)
+    attn, lse, attn_send = attend(low, high, holder, query, kv_own, kv_oth, kpos, meta, chips)
+    attn_got = lax.all_to_all(attn_send, "ctx", 0, 0, tiled=True)
+    attn_low = (
+        attn_got.reshape(seqs, GROUPS, span_rows, feats)
+        .transpose(0, 2, 1, 3)
+        .reshape(seqs * span_rows, width)
+    )
+
+    tokens = tokens_low.reshape(seqs * span_rows, width).astype(f32)
+    cotangent = cot_low.reshape(seqs * span_rows, width).astype(f32)
+    branch = dot(attn_low, weight_out, ((1,), (0,))) + bias_out
+    resid = tokens + branch_scale * branch
+    normed_two = layer_norm(resid, gain_two, shift_two).astype(bf16)
+    hidden = dot(normed_two, weight_fc, ((1,), (0,))) + bias_fc
+    hidden_low = gelu_tanh(hidden).astype(bf16)
+    d_mlp = (branch_scale * cotangent).astype(bf16)
+    grad_proj = own_rows_sum(hidden_low, d_mlp, w)
+    mlp = dot(hidden_low, weight_proj, ((1,), (0,))) + bias_proj
+    block_out = (resid + branch_scale * mlp).astype(bf16)
+
+    d_hidden = dot(d_mlp, weight_proj, ((1,), (1,)))
+    gelu_unused, gelu_pull = jax.vjp(gelu_tanh, hidden)
+    d_pre = gelu_pull(d_hidden)[0].astype(bf16)
+    d_normed_two = dot(d_pre, weight_fc, ((1,), (1,)))
+    d_part, unit_two = norm_back(d_normed_two, resid, gain_two)
+    d_resid = cotangent + d_part
+    d_branch = (branch_scale * d_resid).astype(bf16)
+    d_attn = dot(d_branch, weight_out, ((1,), (1,))).astype(bf16)
+    d_send = (
+        d_attn.reshape(seqs, span_rows, GROUPS, feats)
+        .transpose(0, 2, 1, 3)
+        .reshape(chips, span_rows, feats)
+    )
+    d_got = lax.all_to_all(d_send, "ctx", 0, 0, tiled=True)
+    grad_fc = own_rows_sum(normed_two, d_pre, w)
+    grad_out = own_rows_sum(attn_low, d_branch, w)
+
+    def total(value):
+        return jnp.sum(value.astype(f32), axis=0)
+
+    sums = jnp.concatenate(
+        [
+            total(d_branch),
+            total(d_normed_two * unit_two),
+            total(d_normed_two),
+            total(d_mlp),
+            total(d_pre),
+        ]
+    )
+    sums = sum_everywhere(sums.reshape(-1, 128)).reshape(-1)
+
+    grad_proj = gather_pair(reduce_pair(*column_halves(grad_proj), where), where)
+    grad_fc = gather_pair(reduce_pair(*column_halves(grad_fc), where), where)
+    grad_out = gather_pair(reduce_pair(*column_halves(grad_out), where), where)
+
+    d_query, d_own, d_oth = attend_back(
+        low, high, holder, query, kv_own, kv_oth, kpos, meta, d_got, attn, lse
+    )
+    d_recv = other_core(d_oth)
+    d_pieces, d_qkv, part_gain, part_shift, part_bias = unproject(
+        order, pieces, d_query, d_own, d_recv, weight_in
+    )
+    grad_in = own_rows_sum(normed_one, d_qkv, w)
+    grad_in = jnp.concatenate([grad_in[:, PAD * i : PAD * i + feats] for i in range(3)], axis=1)
+    shard = reduce_z(grad_in, z)
+    shards = [shard] + [send_z(shard, k) for k in (1, 2, 3)]
+    block = jnp.concatenate([row(jnp.stack(shards), (z - i) % 4) for i in range(4)], axis=0)
+    top, bottom = block[: half // 2], block[half // 2 :]
+    top_x, bottom_y = send_x(top), send_y(bottom)
+    top_y, bottom_x = send_y(top), send_x(bottom)
+    top_xy, bottom_xy = send_y(top_x), send_x(bottom_y)
+    tops = jnp.stack([top, top_x, top_y, top_xy])
+    bottoms = jnp.stack([bottom, bottom_x, bottom_y, bottom_xy])
+    by_group = [
+        jnp.concatenate([row(tops, group ^ g), row(bottoms, group ^ g)], axis=0) for g in range(GROUPS)
+    ]
+    grad_w_qkv = jnp.concatenate(
+        [by_group[g][:, feats * i : feats * (i + 1)] for i in range(3) for g in range(GROUPS)], axis=1
+    ).astype(f32)
+    zeros = jnp.zeros((1, width), f32)
+    parts = jnp.concatenate(
+        [
+            part_gain,
+            part_shift,
+            lax.dynamic_update_slice(zeros, part_bias[:, :feats], (0, group * feats)),
+            lax.dynamic_update_slice(zeros, part_bias[:, 2 * PAD : 2 * PAD + feats], (0, group * feats)),
+        ],
+        axis=0,
+    )
+    parts = sum_everywhere(parts.reshape(-1, 128)).reshape(4, width)
+
+    left, right = d_pieces[:8], d_pieces[8:]
+    left = sum_low(left[:4], send_y(left[4:]))
+    right = sum_low(right[:4], send_x(right[4:]))
+    left = sum_low(left[:2], send_x(left[2:]))
+    right = sum_low(right[:2], send_y(right[2:]))
+    got = [left[0], send_z(left[1], 3), send_z(right[0], 2), send_z(right[1], 1)]
+    got = jnp.stack(got)
+    d_normed_one = jnp.stack([row(got, (s - z) % 4) for s in range(seqs)])
+    d_normed_one = d_normed_one.reshape(seqs * span_rows, width).astype(f32)
+    d_first, unused = norm_back(d_normed_one, tokens, gain_one)
+    d_input = d_resid + d_first
+
+    def mine(value, size=half):
+        return lax.dynamic_slice_in_dim(value, w * size, size, 0)
+
     return (
-        0.5
-        * values
-        * (1.0 + jnp.tanh(0.7978845608028654 * (values + 0.044715 * values * values * values)))
+        give_spans(block_out.reshape(seqs, span_rows, width)),
+        give_spans(d_input.reshape(seqs, span_rows, width)),
+        mine(parts[0]),
+        mine(parts[1]),
+        grad_w_qkv,
+        jnp.stack([mine(parts[2]), mine(parts[3])]),
+        grad_out,
+        mine(sums[:width]),
+        mine(sums[width : 2 * width]),
+        mine(sums[2 * width : 3 * width]),
+        grad_fc,
+        mine(sums[4 * width :], fc_bias.shape[0]),
+        grad_proj,
+        mine(sums[3 * width : 4 * width]),
     )
 
 
@@ -456,8 +1206,9 @@
         P("wt"),
         P("wt", "ctx", None),
     )
+    fast = dict(mesh.shape) == {"ctx": 16, "wt": 2}
     return jax.shard_map(
-        per_device,
+        by_owner if fast else per_device,
         mesh=mesh,
         in_specs=placed,
         out_specs=(

time: 1340 us -> 499 us (0.37)
  blocking collectives: 757 us -> 0 us
  matrix products: 204 us -> 36.8 us
  starting transfers between devices: 0.86 us -> 113 us
  Pallas kernels: 0 us -> 70.3 us
  local copies, waits for them, and re-layouts: 108 us -> 39.2 us
  other arithmetic: 40.3 us -> 25.9 us
    psum x1 -> x0, blocking collectives: 583 us -> none  [per_device(): lax.psum((shares[0], shares[1], shares[2], shares[3], shares[4], shares[5...]
    all_gather x8 -> x3, waiting for transfers between devices: 191 us -> 0.04 us  [the longest x1 0.02 us: by_owner(): weight_out = lax.all_gather(w_out, 'wt', axis=0, tiled=True)]
    ppermute x0 -> x99, waiting for transfers between devices: none -> 174 us  [the longest x36 78.8 us: send_z(): return lax.ppermute(value, 'ctx', z_shift(step))]
    all_gather x10 -> x0, blocking collectives: 170 us -> none  [the longest x1 88.6 us: per_device(): lax.all_gather(delta, 'ctx', axis=1, tiled=True)]
    dot_general x33 -> x14, matrix products: 204 us -> 36.8 us  [dot(): lax.dot_general(left, right, (dims, ((), ())), preferred_element_type=f32)]
    ppermute x0 -> x99, starting transfers between devices: none -> 102 us  [the longest x36 46.1 us: send_z(): return lax.ppermute(value, 'ctx', z_shift(step))]
    pallas_call x0 -> x7, Pallas kernels: none -> 70.3 us  [the longest x1 22.8 us: attend_back(): pl.pallas_call(attend_back_kernel, grid_spec=grid_spec, out_shape=[jax.Sh...]
    dynamic_slice x36 -> x14, local copies, waits for them, and re-layouts: 63.3 us -> 5 us  [the longest x9 4.72 us: mine(): return lax.dynamic_slice_in_dim(value, w * size, size, 0)]
  transfers between devices with their start and end apart: 13 -> 104, of which waited for: 3 -> 45; matrix products, arithmetic and copies ran while one was open for 26% -> 17% of each run, Pallas kernels for 0% -> 13%
where the time goes in v1:
time: 499 us; the launch traced here: 492 us
  waiting for transfers between devices  188 us (38%)
  starting transfers between devices  113 us (23%)
  Pallas kernels  70.3 us (14%)
  local copies, waits for them, and re-layouts  39.2 us (8%)
  matrix products  36.8 us (7%)
  other arithmetic  25.9 us (5%)
  between operations  18.1 us (4%)
    ppermute x36, waiting for transfers between devices, send_z(): return lax.ppermute(value, 'ctx', z_shift(step))  78.8 us
    ppermute x24, waiting for transfers between devices, send_y(): return lax.ppermute(value, 'ctx', y_pairs)  55.9 us
    ppermute x36, starting transfers between devices, send_z(): return lax.ppermute(value, 'ctx', z_shift(step))  46.1 us
    ppermute x24, waiting for transfers between devices, send_x(): return lax.ppermute(value, 'ctx', x_pairs)  38.9 us
    dot_general x14, matrix products, dot(): lax.dot_general(left, right, (dims, ((), ())), preferred_element_type=f32)  36.8 us
    ppermute x24, starting transfers between devices, send_y(): return lax.ppermute(value, 'ctx', y_pairs)  26.8 us
    pallas_call x1, Pallas kernels, attend_back(): pl.pallas_call(attend_back_kernel, grid_spec=grid_spec, out_shape=[jax.Sh...  22.8 us
    ppermute x24, starting transfers between devices, send_x(): return lax.ppermute(value, 'ctx', x_pairs)  22 us
  transfers between devices with their start and end apart: 104, of which 45 were waited for; matrix products, arithmetic and copies ran while one was open for 17% of the time, Pallas kernels for 13%

profile of v1, /device:TPU:0, one launch (start us, length us, event | category | flops | bytes accessed | tf_op | source)
XLA Modules:
  0.0 491.6 jit_solution(13011439000951719454)
XLA Ops:
  48.8 4.5 collective-permute-done.7
  56.4 6.0 %collective-permute-done.4 = bf16[4,72,768]{2,1,0:T(8,128)(2,1)S(1)} collective-permute-done((bf16[4,72,768]{2,1,0:T(8,128)(2,1)S(1)}, bf16[4,72,768]{2,1,0:T(8,128)(2,1)S(1)}, u32[]{:S(2)}, u32[]{:S(2)}) %collective-permute-start.4) | collective-permute-done | bytes 442400 | tf_op jit(solution)/shard_map/ppermute | solution.py:41
  66.1 6.5 %project.1 = (bf16[1152,768]{1,0:T(8,128)(2,1)}, bf16[1152,256]{1,0:T(8,128)(2,1)}, bf16[1152,512]{1,0:T(8,128)(2,1)}) custom-call(s32[16]{0:T(128)} %compare_select_fusion.7.order_ref, bf16[16,72,768]{2,1,0:T(8,128)(2,1)} %copy-done, bf16[16,72,768]{2,1,0:T(8,128)(2,1)} %copy-done, bf16[16,72,768]{2,1,0:T(8,128)(2,1)} %copy-done, ...), custom_call_target="tpu_custom_call" | custom-call | flops 1358954496 | bytes 6291456 | tf_op jit(solution)/shard_map/project/pallas_call | solution.py:116
  77.1 20.8 %attend.1 = (f32[1152,256]{1,0:T(8,128)}, f32[9,1,384]{2,1,0:T(1,128)}, bf16[16,72,192]{2,1,0:T(8,128)(2,1)}) custom-call(s32[9]{0:T(128)} %get-tuple-element.170.low_ref, s32[9]{0:T(128)} %get-tuple-element.169.high_ref, s32[16]{0:T(128)} %copy-done.47, bf16[1152,256]{1,0:T(8,128)(2,1)} %get-tuple-element.28.q_ref, ...), custom_call_target="tpu_custom_call" | custom-call | flops 2038431744 | bytes 8388608 | tf_op jit(solution)/shard_map/attend/pallas_call | solution.py:222
  97.9 7.2 %all-to-all-start = ((bf16[16,72,192]{2,1,0:T(8,128)(2,1)}), bf16[16,72,192]{2,1,0:T(8,128)(2,1)S(1)}, u32[]{:S(2)}, u32[]{:S(2)}) async-start(bf16[16,72,192]{2,1,0:T(8,128)(2,1)} %get-tuple-element.30), calls=%async_computation | async-start | bytes 1179648 | tf_op jit(solution)/shard_map/all_to_all | solution.py:655
  106.6 12.4 %all-to-all-done = bf16[16,72,192]{2,1,0:T(8,128)(2,1)S(1)} async-done(((bf16[16,72,192]{2,1,0:T(8,128)(2,1)}), bf16[16,72,192]{2,1,0:T(8,128)(2,1)S(1)}, u32[]{:S(2)}, u32[]{:S(2)}) %all-to-all-start) | async-done | bytes 442400 | tf_op jit(solution)/shard_map/all_to_all | solution.py:655
  122.2 5.8 %convolution_add_fusion = f32[288,3072]{1,0:T(8,128)} fusion(bf16[288,768]{1,0:T(8,128)(2,1)S(1)} %add_convert_fusion.5, bf16[768,3072]{1,0:T(8,128)(2,1)} %all-gather.6.cloned.1.call-done, f32[3072]{0:T(1024)S(1)} %add.747), kind=kOutput, calls=%fused_computation.7 | convolution fusion | flops 1359839232 | bytes 8712192 | tf_op jit(solution)/shard_map/dot_general | solution.py:65
  128.0 8.3 %convert_reduce_fusion = (f32[3072]{0:T(1024)S(1)}, bf16[288,3072]{1,0:T(8,128)(2,1)S(1)}, bf16[288,3072]{1,0:T(8,128)(2,1)S(1)}) fusion(f32[288,3072]{1,0:T(8,128)} %convolution_add_fusion, bf16[288,768]{1,0:T(8,128)(2,1)S(1)} %fusion.21, bf16[3072,768]{1,0:T(8,128)(2,1)} %all-gather.8.cloned.1.call-done), kind=kOutput, calls=%fused_computation.14 | convolution fusion | flops 1383724032 | bytes 12251136 | tf_op jit(solution)/shard_map/dot_general | solution.py:65
  143.0 3.7 collective-permute-start.42
  163.1 3.8 collective-permute-start.64
  172.7 7.2 %collective-permute-done.63 = f32[48,128]{1,0:T(8,128)S(1)} collective-permute-done((f32[48,128]{1,0:T(8,128)S(1)}, f32[48,128]{1,0:T(8,128)S(1)}, u32[]{:S(2)}, u32[]{:S(2)}) %collective-permute-start.63) | collective-permute-done | bytes 24608 | tf_op jit(solution)/shard_map/ppermute | solution.py:45
  187.9 22.8 %attend_back.1 = (bf16[1152,256]{1,0:T(8,128)(2,1)}, f32[1152,512]{1,0:T(8,128)}, bf16[1152,512]{1,0:T(8,128)(2,1)}) custom-call(s32[9]{0:T(128)} %get-tuple-element.170.low_ref, s32[9]{0:T(128)} %get-tuple-element.169.high_ref, s32[16]{0:T(128)} %copy-done.47, bf16[1152,256]{1,0:T(8,128)(2,1)} %get-tuple-element.28.q_ref, ...), custom_call_target="tpu_custom_call" | custom-call | flops 5096079360 | bytes 12582912 | tf_op jit(solution)/shard_map/attend_back/pallas_call | solution.py:332
  228.2 7.7 %unproject.1 = (bf16[16,72,768]{2,1,0:T(8,128)(2,1)}, bf16[1152,768]{1,0:T(8,128)(2,1)}, f32[1,768]{1,0:T(1,128)}, f32[1,768]{1,0:T(1,128)}, f32[1,768]{1,0:T(1,128)}) custom-call(s32[16]{0:T(128)} %compare_select_fusion.7.order_ref, bf16[16,72,768]{2,1,0:T(8,128)(2,1)} %copy-done, bf16[16,72,768]{2,1,0:T(8,128)(2,1)} %copy-done, ...), custom_call_target="tpu_custom_call" | custom-call | flops 1358954496 | bytes 9437184 | tf_op jit(solution)/shard_map/unproject/pallas_call | solution.py:396
  284.2 20.5 %collective-permute-done.19 = bf16[2,72,768]{2,1,0:T(8,128)(2,1)S(1)} collective-permute-done((bf16[2,72,768]{2,1,0:T(8,128)(2,1)S(1)}, bf16[2,72,768]{2,1,0:T(8,128)(2,1)S(1)}, u32[]{:S(2)}, u32[]{:S(2)}) %collective-permute-start.19) | collective-permute-done | bytes 221216 | tf_op jit(solution)/shard_map/ppermute | solution.py:41
  308.5 11.0 %collective-permute-done.31 = bf16[96,576]{1,0:T(8,128)(2,1)S(1)} collective-permute-done((bf16[96,576]{1,0:T(8,128)(2,1)S(1)}, bf16[96,576]{1,0:T(8,128)(2,1)S(1)}, u32[]{:S(2)}, u32[]{:S(2)}) %collective-permute-start.31) | collective-permute-done | bytes 110624 | tf_op jit(solution)/shard_map/ppermute | solution.py:45
  319.6 4.4 collective-permute-start.35
  333.5 4.9 collective-permute-done.34
  342.9 16.0 %collective-permute-done.83 = bf16[768,384]{1,0:T(8,128)(2,1)S(1)} collective-permute-done((bf16[768,384]{1,0:T(8,128)(2,1)S(1)}, bf16[768,384]{1,0:T(8,128)(2,1)S(1)}, u32[]{:S(2)}, u32[]{:S(2)}) %collective-permute-start.83) | collective-permute-done | bytes 589856 | tf_op jit(solution)/shard_map/ppermute | solution.py:37
  365.7 8.9 %collective-permute-done.69 = bf16[96,1536]{1,0:T(8,128)(2,1)S(1)} collective-permute-done((bf16[96,1536]{1,0:T(8,128)(2,1)S(1)}, bf16[96,1536]{1,0:T(8,128)(2,1)S(1)}, u32[]{:S(2)}, u32[]{:S(2)}) %collective-permute-start.69) | collective-permute-done | bytes 294944 | tf_op jit(solution)/shard_map/ppermute | solution.py:37
  376.0 8.0 %collective-permute-done.67 = bf16[96,1536]{1,0:T(8,128)(2,1)S(1)} collective-permute-done((bf16[96,1536]{1,0:T(8,128)(2,1)S(1)}, bf16[96,1536]{1,0:T(8,128)(2,1)S(1)}, u32[]{:S(2)}, u32[]{:S(2)}) %collective-permute-start.67) | collective-permute-done | bytes 294944 | tf_op jit(solution)/shard_map/ppermute | solution.py:41
  394.0 4.3 collective-permute-start.71
  402.6 14.0 %collective-permute-done.71 = bf16[24,3072]{1,0:T(8,128)(2,1)S(1)} collective-permute-done((bf16[24,3072]{1,0:T(8,128)(2,1)S(1)}, bf16[24,3072]{1,0:T(8,128)(2,1)S(1)}, u32[]{:S(2)}, u32[]{:S(2)}) %collective-permute-start.71) | collective-permute-done | bytes 147488 | tf_op jit(solution)/shard_map/ppermute | solution.py:45
  416.7 3.9 collective-permute-start.75
  420.6 9.9 %collective-permute-done.88 = bf16[96,768]{1,0:T(8,128)(2,1)S(1)} collective-permute-done((bf16[96,768]{1,0:T(8,128)(2,1)S(1)}, bf16[96,768]{1,0:T(8,128)(2,1)S(1)}, u32[]{:S(2)}, u32[]{:S(2)}) %collective-permute-start.88) | collective-permute-done | bytes 147488 | tf_op jit(solution)/shard_map/ppermute | solution.py:45
  430.6 3.9 collective-permute-start.92
  434.4 3.8 collective-permute-done.74
  439.7 6.1 %collective-permute-done.91 = bf16[96,768]{1,0:T(8,128)(2,1)S(1)} collective-permute-done((bf16[96,768]{1,0:T(8,128)(2,1)S(1)}, bf16[96,768]{1,0:T(8,128)(2,1)S(1)}, u32[]{:S(2)}, u32[]{:S(2)}) %collective-permute-start.91) | collective-permute-done | bytes 147488 | tf_op jit(solution)/shard_map/ppermute | solution.py:45
  450.2 5.5 %collective-permute-done.77.refs_2_ = bf16[4,24,1536]{2,1,0:T(8,128)(2,1)S(1)} collective-permute-done((bf16[4,24,1536]{2,1,0:T(8,128)(2,1)S(1)}, bf16[4,24,1536]{2,1,0:T(8,128)(2,1)S(1)}, u32[]{:S(2)}, u32[]{:S(2)}) %collective-permute-start.77) | collective-permute-done | bytes 294944 | tf_op jit(solution)/shard_map/ppermute | solution.py:41
  458.3 3.7 collective-permute-done.80.refs_6_
  462.1 3.9 collective-permute-done.94.refs_2_
  475.1 4.7 place.4
  479.9 4.7 place.5
  (523 shorter events, 214.6 us)
Async XLA Ops:
  7.3 112.4 %all-gather.4.cloned.1.call-start = ((), (), s32[]{:S(2)}) async-start(), calls=%async_computation.2 | async-start | bytes 1769472 | tf_op jit(solution)/shard_map/all_gather | solution.py:648
  8.0 114.1 %all-gather.6.cloned.1.call-start = ((), (), s32[]{:S(2)}) async-start(), calls=%async_computation.3 | async-start | bytes 7077888 | tf_op jit(solution)/shard_map/all_gather | solution.py:649
  8.8 119.2 %all-gather.8.cloned.1.call-start = ((), (), s32[]{:S(2)}) async-start(), calls=%async_computation.4 | async-start | bytes 7077888 | tf_op jit(solution)/shard_map/all_gather | solution.py:650
  21.4 51.2 %collective-permute-start.1 = (s32[2,4]{1,0:T(2,128)}, s32[2,4]{1,0:T(2,128)}, u32[]{:S(2)}, u32[]{:S(2)}) collective-permute-start(s32[2,4]{1,0:T(2,128)} %param.18), channel_id=1, source_target_pairs={{0,1},{1,0},{2,3},{3,2},{4,5},{5,4},{6,7},{7,6},{8,9},{9,8},{10,11... | collective-permute-start | bytes 104 | tf_op jit(solution)/shard_map/ppermute | solution.py:33
  26.7 28.2 %collective-permute-start.10 = (bf16[384,768]{1,0:T(8,128)(2,1)S(1)}, bf16[384,768]{1,0:T(8,128)(2,1)S(1)}, u32[]{:S(2)}, u32[]{:S(2)}) collective-permute-start(bf16[384,768]{1,0:T(8,128)(2,1)S(1)} %copy.55), channel_id=1, source_target_pairs={{0,1},{1,0},{2,3},{3,2},{4,5},{5,4},{6,7},{7,6},{8,9},{9,8},{10,11... | collective-permute-start | bytes 1769480 | tf_op jit(solution)/shard_map/ppermute | solution.py:33
  45.0 61.3 %collective-permute-start.13 = (bf16[2,72,768]{2,1,0:T(8,128)(2,1)S(1)}, bf16[2,72,768]{2,1,0:T(8,128)(2,1)S(1)}, u32[]{:S(2)}, u32[]{:S(2)}) collective-permute-start(bf16[2,72,768]{2,1,0:T(8,128)(2,1)S(1)} %get-tuple-element.118), channel_id=1, source_target_pairs={{0,1},{1,0},{2,3},{3,2},{4,5},{5,4},{6,7},{7,6},{8,9},{9,8},{10,11... | collective-permute-start | bytes 663560 | tf_op jit(solution)/shard_map/ppermute | solution.py:33
  97.9 21.0 %all-to-all-start = ((bf16[16,72,192]{2,1,0:T(8,128)(2,1)}), bf16[16,72,192]{2,1,0:T(8,128)(2,1)S(1)}, u32[]{:S(2)}, u32[]{:S(2)}) async-start(bf16[16,72,192]{2,1,0:T(8,128)(2,1)} %get-tuple-element.30), calls=%async_computation | async-start | bytes 1179648 | tf_op jit(solution)/shard_map/all_to_all | solution.py:655
  143.0 25.0 %collective-permute-start.42 = (bf16[384,768]{1,0:T(8,128)(2,1)S(1)}, bf16[384,768]{1,0:T(8,128)(2,1)}, u32[]{:S(2)}, u32[]{:S(2)}) collective-permute-start(bf16[384,768]{1,0:T(8,128)(2,1)S(1)} %convolution_convert_fusion.2), channel_id=1, source_target_pairs={{0,1},{1,0},{2,3},{3,2},{4,5},{5,4},{6,7},{7,6},{8,9},{9,8},{10,11... | collective-permute-start | bytes 1769480 | tf_op jit(solution)/shard_map/ppermute | solution.py:33
  146.9 120.3 %collective-permute-start.65 = (bf16[384,3072]{1,0:T(8,128)(2,1)}, bf16[384,3072]{1,0:T(8,128)(2,1)}, u32[]{:S(2)}, u32[]{:S(2)}) collective-permute-start(bf16[384,3072]{1,0:T(8,128)(2,1)} %convolution_convert_fusion), channel_id=1, source_target_pairs={{0,1},{1,0},{2,3},{3,2},{4,5},{5,4},{6,7},{7,6},{8,9},{9,8},{10,11... | collective-permute-start | bytes 7077896 | tf_op jit(solution)/shard_map/ppermute | solution.py:33
  159.4 27.6 %all-to-all-start.1 = ((bf16[16,72,192]{2,1,0:T(8,128)(2,1)}), bf16[16,72,192]{2,1,0:T(8,128)(2,1)S(1)}, u32[]{:S(2)}, u32[]{:S(2)}) async-start(bf16[16,72,192]{2,1,0:T(8,128)(2,1)} %bitcast.32), calls=%async_computation.1 | async-start | bytes 1179648 | tf_op jit(solution)/shard_map/all_to_all | solution.py:687
  185.7 26.9 %collective-permute-start.44 = (bf16[96,384]{1,0:T(8,128)(2,1)S(1)}, bf16[96,384]{1,0:T(8,128)(2,1)S(1)}, u32[]{:S(2)}, u32[]{:S(2)}) collective-permute-start(bf16[96,384]{1,0:T(8,128)(2,1)S(1)} %dynamic-slice_bitcast_fusion.36), channel_id=1, source_target_pairs={{0,4},{2,6},{4,0},{6,2},{8,12},{10,14},{12,8},{14,10},{16,20},{18,... | collective-permute-start | bytes 221192 | tf_op jit(solution)/shard_map/ppermute | solution.py:41
  242.4 29.9 %collective-permute-start.82 = (bf16[1536,768]{1,0:T(8,128)(2,1)}, bf16[1536,768]{1,0:T(8,128)(2,1)}, u32[]{:S(2)}, u32[]{:S(2)}) collective-permute-start(bf16[1536,768]{1,0:T(8,128)(2,1)} %convolution_convert_fusion.1), channel_id=1, source_target_pairs={{0,1},{1,0},{2,3},{3,2},{4,5},{5,4},{6,7},{7,6},{8,9},{9,8},{10,11... | collective-permute-start | bytes 7077896 | tf_op jit(solution)/shard_map/ppermute | solution.py:33
  260.3 19.2 %collective-permute-start.15 = (bf16[4,72,768]{2,1,0:T(8,128)(2,1)S(1)}, bf16[4,72,768]{2,1,0:T(8,128)(2,1)S(1)}, u32[]{:S(2)}, u32[]{:S(2)}) collective-permute-start(bf16[4,72,768]{2,1,0:T(8,128)(2,1)S(1)} %get-tuple-element.66), channel_id=1, source_target_pairs={{0,4},{2,6},{4,0},{6,2},{8,12},{10,14},{12,8},{14,10},{16,20},{18,... | collective-permute-start | bytes 1327112 | tf_op jit(solution)/shard_map/ppermute | solution.py:41
  271.3 88.5 %collective-permute-start.68 = (bf16[192,1536]{1,0:T(8,128)(2,1)}, bf16[192,1536]{1,0:T(8,128)(2,1)}, u32[]{:S(2)}, u32[]{:S(2)}) collective-permute-start(bf16[192,1536]{1,0:T(8,128)(2,1)} %dynamic-slice_bitcast_fusion.2), channel_id=1, source_target_pairs={{0,4},{2,6},{4,0},{6,2},{8,12},{10,14},{12,8},{14,10},{16,20},{18,... | collective-permute-start | bytes 1769480 | tf_op jit(solution)/shard_map/ppermute | solution.py:41
  276.7 63.6 %collective-permute-start.85 = (bf16[768,384]{1,0:T(8,128)(2,1)}, bf16[768,384]{1,0:T(8,128)(2,1)}, u32[]{:S(2)}, u32[]{:S(2)}) collective-permute-start(bf16[768,384]{1,0:T(8,128)(2,1)} %dynamic-slice_bitcast_fusion), channel_id=1, source_target_pairs={{0,4},{2,6},{4,0},{6,2},{8,12},{10,14},{12,8},{14,10},{16,20},{18,... | collective-permute-start | bytes 1769480 | tf_op jit(solution)/shard_map/ppermute | solution.py:41
  279.8 24.9 %collective-permute-start.19 = (bf16[2,72,768]{2,1,0:T(8,128)(2,1)S(1)}, bf16[2,72,768]{2,1,0:T(8,128)(2,1)S(1)}, u32[]{:S(2)}, u32[]{:S(2)}) collective-permute-start(bf16[2,72,768]{2,1,0:T(8,128)(2,1)S(1)} %slice.382), channel_id=1, source_target_pairs={{0,4},{2,6},{4,0},{6,2},{8,12},{10,14},{12,8},{14,10},{16,20},{18,... | collective-permute-start | bytes 663560 | tf_op jit(solution)/shard_map/ppermute | solution.py:41
  280.9 24.3 %collective-permute-start.16 = (bf16[2,72,768]{2,1,0:T(8,128)(2,1)S(1)}, bf16[2,72,768]{2,1,0:T(8,128)(2,1)S(1)}, u32[]{:S(2)}, u32[]{:S(2)}) collective-permute-start(bf16[2,72,768]{2,1,0:T(8,128)(2,1)S(1)} %slice.378), channel_id=1, source_target_pairs={{0,2},{2,0},{4,6},{6,4},{8,10},{10,8},{12,14},{14,12},{16,18},{18,... | collective-permute-start | bytes 663560 | tf_op jit(solution)/shard_map/ppermute | solution.py:37
  283.5 23.1 %collective-permute-start.32 = (bf16[96,576]{1,0:T(8,128)(2,1)S(1)}, bf16[96,576]{1,0:T(8,128)(2,1)S(1)}, u32[]{:S(2)}, u32[]{:S(2)}) collective-permute-start(bf16[96,576]{1,0:T(8,128)(2,1)S(1)} %get-tuple-element.112), channel_id=1, source_target_pairs={{0,24},{2,26},{4,28},{6,30},{8,0},{10,2},{12,4},{14,6},{16,8},{18,... | collective-permute-start | bytes 331784 | tf_op jit(solution)/shard_map/ppermute | solution.py:45
  332.7 29.7 %collective-permute-start.66 = (bf16[192,1536]{1,0:T(8,128)(2,1)S(1)}, bf16[192,1536]{1,0:T(8,128)(2,1)S(1)}, u32[]{:S(2)}, u32[]{:S(2)}) collective-permute-start(bf16[192,1536]{1,0:T(8,128)(2,1)S(1)} %copy-done.16), channel_id=1, source_target_pairs={{0,2},{2,0},{4,6},{6,4},{8,10},{10,8},{12,14},{14,12},{16,18},{18,... | collective-permute-start | bytes 1769480 | tf_op jit(solution)/shard_map/ppermute | solution.py:37
  338.4 20.5 %collective-permute-start.83 = (bf16[768,384]{1,0:T(8,128)(2,1)S(1)}, bf16[768,384]{1,0:T(8,128)(2,1)S(1)}, u32[]{:S(2)}, u32[]{:S(2)}) collective-permute-start(bf16[768,384]{1,0:T(8,128)(2,1)S(1)} %copy-done.17), channel_id=1, source_target_pairs={{0,2},{2,0},{4,6},{6,4},{8,10},{10,8},{12,14},{14,12},{16,18},{18,... | collective-permute-start | bytes 1769480 | tf_op jit(solution)/shard_map/ppermute | solution.py:37
  339.1 24.9 %collective-permute-start.22 = (f32[2,72,768]{2,1,0:T(8,128)S(1)}, f32[2,72,768]{2,1,0:T(8,128)S(1)}, u32[]{:S(2)}, u32[]{:S(2)}) collective-permute-start(f32[2,72,768]{2,1,0:T(8,128)S(1)} %bitcast.384), channel_id=1, source_target_pairs={{0,1},{1,0},{2,3},{3,2},{4,5},{5,4},{6,7},{7,6},{8,9},{9,8},{10,11... | collective-permute-start | bytes 1327112 | tf_op jit(solution)/shard_map/ppermute | solution.py:33
  340.4 43.9 %collective-permute-start.40 = (bf16[192,576]{1,0:T(8,128)(2,1)S(1)}, bf16[192,576]{1,0:T(8,128)(2,1)S(1)}, u32[]{:S(2)}, u32[]{:S(2)}) collective-permute-start(bf16[192,576]{1,0:T(8,128)(2,1)S(1)} %get-tuple-element.132), channel_id=1, source_target_pairs={{0,4},{2,6},{4,0},{6,2},{8,12},{10,14},{12,8},{14,10},{16,20},{18,... | collective-permute-start | bytes 663560 | tf_op jit(solution)/shard_map/ppermute | solution.py:41
  358.9 35.1 %collective-permute-start.39 = (bf16[192,576]{1,0:T(8,128)(2,1)S(1)}, bf16[192,576]{1,0:T(8,128)(2,1)S(1)}, u32[]{:S(2)}, u32[]{:S(2)}) collective-permute-start(bf16[192,576]{1,0:T(8,128)(2,1)S(1)} %get-tuple-element.132), channel_id=1, source_target_pairs={{0,2},{2,0},{4,6},{6,4},{8,10},{10,8},{12,14},{14,12},{16,18},{18,... | collective-permute-start | bytes 663560 | tf_op jit(solution)/shard_map/ppermute | solution.py:37
  359.9 25.8 %collective-permute-start.36 = (bf16[192,576]{1,0:T(8,128)(2,1)S(1)}, bf16[192,576]{1,0:T(8,128)(2,1)S(1)}, u32[]{:S(2)}, u32[]{:S(2)}) collective-permute-start(bf16[192,576]{1,0:T(8,128)(2,1)S(1)} %get-tuple-element.134), channel_id=1, source_target_pairs={{0,2},{2,0},{4,6},{6,4},{8,10},{10,8},{12,14},{14,12},{16,18},{18,... | collective-permute-start | bytes 663560 | tf_op jit(solution)/shard_map/ppermute | solution.py:37
  362.4 83.6 %collective-permute-start.37 = (bf16[192,576]{1,0:T(8,128)(2,1)S(1)}, bf16[192,576]{1,0:T(8,128)(2,1)S(1)}, u32[]{:S(2)}, u32[]{:S(2)}) collective-permute-start(bf16[192,576]{1,0:T(8,128)(2,1)S(1)} %get-tuple-element.134), channel_id=1, source_target_pairs={{0,4},{2,6},{4,0},{6,2},{8,12},{10,14},{12,8},{14,10},{16,20},{18,... | collective-permute-start | bytes 663560 | tf_op jit(solution)/shard_map/ppermute | solution.py:41
  390.8 57.3 %collective-permute-start.38 = (bf16[192,576]{1,0:T(8,128)(2,1)S(1)}, bf16[192,576]{1,0:T(8,128)(2,1)S(1)}, u32[]{:S(2)}, u32[]{:S(2)}) collective-permute-start(bf16[192,576]{1,0:T(8,128)(2,1)S(1)} %collective-permute-done.36), channel_id=1, source_target_pairs={{0,4},{2,6},{4,0},{6,2},{8,12},{10,14},{12,8},{14,10},{16,20},{18,... | collective-permute-start | bytes 663560 | tf_op jit(solution)/shard_map/ppermute | solution.py:41
  394.0 22.5 %collective-permute-start.71 = (bf16[24,3072]{1,0:T(8,128)(2,1)S(1)}, bf16[24,3072]{1,0:T(8,128)(2,1)S(1)}, u32[]{:S(2)}, u32[]{:S(2)}) collective-permute-start(bf16[24,3072]{1,0:T(8,128)(2,1)S(1)} %get-tuple-element.89), channel_id=1, source_target_pairs={{0,16},{2,18},{4,20},{6,22},{8,24},{10,26},{12,28},{14,30},{16,0},... | collective-permute-start | bytes 442376 | tf_op jit(solution)/shard_map/ppermute | solution.py:45
  398.4 18.2 %collective-permute-start.70 = (bf16[24,3072]{1,0:T(8,128)(2,1)S(1)}, bf16[24,3072]{1,0:T(8,128)(2,1)S(1)}, u32[]{:S(2)}, u32[]{:S(2)}) collective-permute-start(bf16[24,3072]{1,0:T(8,128)(2,1)S(1)} %get-tuple-element.87), channel_id=1, source_target_pairs={{0,8},{2,10},{4,12},{6,14},{8,16},{10,18},{12,20},{14,22},{16,24},... | collective-permute-start | bytes 442376 | tf_op jit(solution)/shard_map/ppermute | solution.py:45
  448.1 17.9 %collective-permute-start.94 = (bf16[4,96,384]{2,1,0:T(8,128)(2,1)S(1)}, bf16[4,96,384]{2,1,0:T(8,128)(2,1)}, u32[]{:S(2)}, u32[]{:S(2)}) collective-permute-start(bf16[4,96,384]{2,1,0:T(8,128)(2,1)S(1)} %get-tuple-element.81.refs_0_), channel_id=1, source_target_pairs={{0,4},{2,6},{4,0},{6,2},{8,12},{10,14},{12,8},{14,10},{16,20},{18,... | collective-permute-start | bytes 884744 | tf_op jit(solution)/shard_map/ppermute | solution.py:41
  449.6 18.1 %collective-permute-start.96 = (bf16[4,96,384]{2,1,0:T(8,128)(2,1)S(1)}, bf16[4,96,384]{2,1,0:T(8,128)(2,1)}, u32[]{:S(2)}, u32[]{:S(2)}) collective-permute-start(bf16[4,96,384]{2,1,0:T(8,128)(2,1)S(1)} %get-tuple-element.80.refs_4_), channel_id=1, source_target_pairs={{0,2},{2,0},{4,6},{6,4},{8,10},{10,8},{12,14},{14,12},{16,18},{18,... | collective-permute-start | bytes 884744 | tf_op jit(solution)/shard_map/ppermute | solution.py:37
  456.6 23.3 %collective-permute-start.93 = (bf16[4,96,384]{2,1,0:T(8,128)(2,1)S(1)}, bf16[4,96,384]{2,1,0:T(8,128)(2,1)}, u32[]{:S(2)}, u32[]{:S(2)}) collective-permute-start(bf16[4,96,384]{2,1,0:T(8,128)(2,1)S(1)} %get-tuple-element.81.refs_0_), channel_id=1, source_target_pairs={{0,2},{2,0},{4,6},{6,4},{8,10},{10,8},{12,14},{14,12},{16,18},{18,... | collective-permute-start | bytes 884744 | tf_op jit(solution)/shard_map/ppermute | solution.py:37
  462.1 17.8 %collective-permute-start.97 = (bf16[4,96,384]{2,1,0:T(8,128)(2,1)S(1)}, bf16[4,96,384]{2,1,0:T(8,128)(2,1)}, u32[]{:S(2)}, u32[]{:S(2)}) collective-permute-start(bf16[4,96,384]{2,1,0:T(8,128)(2,1)S(1)} %get-tuple-element.80.refs_4_), channel_id=1, source_target_pairs={{0,4},{2,6},{4,0},{6,2},{8,12},{10,14},{12,8},{14,10},{16,20},{18,... | collective-permute-start | bytes 884744 | tf_op jit(solution)/shard_map/ppermute | solution.py:41
  (127 other events, 1087.1 us)
Sparse Core Ops, SparseCore 0:
  9.7 11.9 all-gather.3
  23.2 15.5 all-gather.5
  40.4 15.6 all-gather.7
